TPU v7x, 128 devices: a whole 4x4x4 slice. The times are simulated.
128 devices in a mesh: grp: 4 (over x), blk: 32 (over z, y, core).
Axes of the slice: x: 4, y: 4, z: 4, core: 2. Of those that a mesh axis runs over, the one named last changes fastest.
Arguments:
- activations: bfloat16 [131072, 3072], P(('grp', 'blk')), may hold values from -6 to 6
- out_grads: bfloat16 [131072, 3072], P(('grp', 'blk')), may hold values from -6 to 6
- proj_act: bfloat16 [3072, 128], replicated, may hold values from -1 to 1
- proj_out: bfloat16 [3072, 256], replicated, may hold values from -0.109375 to 0.109375
Outputs:
- scores: float32 [2048, 512], P(('grp', 'blk'))
All inputs are finite; a program needn't handle non-finite values.
Results may differ from a plain program's by a relative error of at most 0.0012.
Values may be sent and summed in bfloat16 or wider, within the bound.
No kernel may reach another device: no remote copies, remote signals or barrier semaphores. Data moves between devices by JAX's collectives and lax.ppermute only.
A program may use at most 64 MiB of HBM per device.

v0:
```python
import math

import jax
import jax.numpy as jnp
from jax import lax
from jax.sharding import Mesh
from jax.sharding import PartitionSpec as P

SEQ = 64
ITERS = 4
BLK = ("blk_0", "blk_1", "blk_2")
GRP_BLK = ("grp", "blk_0", "blk_1", "blk_2")


damping_rate = 0.5
power_steps = 3


def split_up(array, dim, size):
    shape = array.shape
    blocks = array.reshape(*shape[:dim], size, shape[dim] // size, *shape[dim + 1 :])
    return jnp.moveaxis(blocks, dim, 0)


def in_order(blocks, dim):
    shape = list(blocks.shape[1:])
    shape[dim] *= blocks.shape[0]
    return jnp.moveaxis(blocks, 0, dim).reshape(shape)


def moved_by_axis(blocks, axes, turns):
    shape = [lax.axis_size(a) for a in axes]
    blocks = blocks.reshape(*shape, *blocks.shape[1:])
    for k in turns:
        blocks = lax.all_to_all(blocks, axes[k], split_axis=k, concat_axis=k, tiled=True)
    return blocks.reshape(-1, *blocks.shape[len(axes) :])


def core_and_chips(array, groups, turns, split_dim, concat_dim):
    size = lax.axis_size(groups[0]) * lax.axis_size(groups[1])
    blocks = split_up(array, split_dim, size)
    return in_order(moved_by_axis(blocks, groups, turns), concat_dim)


def one_axis_at_a_time(array, axes):
    for axis in axes:
        array = lax.psum(array, axis)
    return array


def sum_at_owner(array, axis, dim):
    size = lax.axis_size(axis)
    blocks = lax.all_to_all(split_up(array, dim, size), axis, 0, 0, tiled=True)
    return jnp.sum(blocks, axis=0)


def top_estimate(gram_sum):
    width = gram_sum.shape[0]
    vector = jnp.full((width,), 1.0 / math.sqrt(width), jnp.float32)
    top = jnp.float32(1.0)
    for step in range(power_steps):
        image = jnp.dot(gram_sum, vector, precision=lax.Precision.HIGHEST)
        top = jnp.sqrt(jnp.sum(image * image) + 1e-06)
        vector = image / top
    return top


def chebyshev(gram_sum, damping, right_side):
    radius = top_estimate(gram_sum)
    center = damping + radius

    def operate(field):
        return jnp.dot(gram_sum, field, precision=lax.Precision.HIGHEST) + damping * field

    stride = 1.0 / center
    direction = right_side
    solution = stride * direction
    residual = right_side - stride * operate(direction)
    for sweep in range(1, ITERS):
        if sweep == 1:
            momentum = 0.5 * (radius * stride) ** 2
        else:
            momentum = (0.5 * radius * stride) ** 2
        stride = 1.0 / (center - momentum / stride)
        direction = residual + momentum * direction
        solution = solution + stride * direction
        if sweep + 1 < ITERS:
            residual = residual - stride * operate(direction)
    return solution


def self_product(rows):
    return lax.dot_general(rows, rows, (((0,), (0,)), ((), ())), preferred_element_type=jnp.float32)


def shards(activations, out_grads, proj_act, proj_out):
    examples = activations.shape[0] // SEQ
    act_low = jnp.dot(activations, proj_act, preferred_element_type=jnp.float32).astype(
        jnp.bfloat16
    )
    grad_low = jnp.dot(out_grads, proj_out, preferred_element_type=jnp.float32).astype(jnp.bfloat16)
    features = jnp.einsum(
        "etr,ets->ers",
        act_low.reshape(examples, SEQ, -1),
        grad_low.reshape(examples, SEQ, -1),
        preferred_element_type=jnp.float32,
    )
    features = features.astype(jnp.bfloat16).reshape(examples, -1)
    block_rows = core_and_chips(features, (("blk_0", "blk_1"), "blk_2"), (0, 1), 1, 0)
    width = block_rows.shape[1]
    widened = block_rows.astype(jnp.float32)
    total = one_axis_at_a_time(jnp.sum(widened * widened), GRP_BLK)
    gram_sum = self_product(lax.all_gather(block_rows, "grp", axis=0, tiled=True))
    damping = damping_rate * total / (width * lax.axis_size(BLK))
    right_side = block_rows.T.astype(jnp.float32)
    solved = chebyshev(gram_sum, damping, right_side).astype(jnp.bfloat16)
    scores = sum_at_owner(jnp.dot(block_rows, solved, preferred_element_type=jnp.float32), BLK, 0)
    return scores * float(examples * lax.axis_size("grp"))


def solution(mesh):
    split = Mesh(
        mesh.devices.reshape(mesh.shape["grp"], 4, 4, 2), ("grp", "blk_0", "blk_1", "blk_2")
    )
    placed = (P(GRP_BLK, None), P(GRP_BLK, None), P(), P())
    return jax.shard_map(
        shards, mesh=split, in_specs=placed, out_specs=P(GRP_BLK, None), check_vma=False
    )
```

profile of v0, /device:TPU:0, one launch (start us, length us, event | category | flops | bytes accessed | tf_op | source)
XLA Modules:
  0.0 179.0 jit_solution(9922667226853044475)
XLA Ops:
  6.5 4.9 %convolution_convert_fusion.2 = bf16[1024,128]{1,0:T(8,128)(2,1)S(1)} fusion(bf16[1024,3072]{1,0:T(8,128)(2,1)} %param.4, bf16[3072,128]{1,0:T(8,128)(2,1)} %param.6), kind=kOutput, calls=%fused_computation.19 | convolution fusion | flops 805437440 | bytes 7340032 | tf_op jit(solution)/shard_map/dot_general | solution.py:98
  11.4 0.4 copy-done.7
  11.8 1.8 %convolution_convert_fusion.1 = bf16[1024,256]{1,0:T(8,128)(2,1)S(1)} fusion(bf16[1024,3072]{1,0:T(8,128)(2,1)S(1)} %copy-done.7, bf16[3072,256]{1,0:T(8,128)(2,1)S(1)} %copy-done), kind=kOutput, calls=%fused_computation.18 | convolution fusion | flops 1610874880 | bytes 8388608 | tf_op jit(solution)/shard_map/dot_general | solution.py:101
  13.6 0.5 convolution_convert_fusion
  14.1 1.5 reshape_reshape.6
  15.6 1.8 %copy.12 = bf16[16,32,1024]{2,0,1:T(8,128)(2,1)S(1)} copy(bf16[16,32,1024]{2,1,0:T(8,128)(2,1)} %reshape_reshape.6) | data formatting | bytes 2097152 | tf_op jit(solution)/shard_map/reshape;reshape | solution.py:21
  17.4 25.1 %all_to_all.15 = bf16[16,2,16,1024]{3,2,1,0:T(8,128)(2,1)S(1)} all-to-all(bf16[16,2,16,1024]{3,2,1,0:T(8,128)(2,1)S(1)} %bitcast.84), channel_id=1, replica_groups=mesh['grp'=4,'blk_0'=4,'blk_1'=4,'blk_2'=2] {'blk_0','blk_1'}, dimensions={0} | all-to-all | bytes 2097152 | tf_op jit(solution)/shard_map/all_to_all | solution.py:35
  42.5 0.1 copy.13
  42.6 4.6 %all_to_all.16 = bf16[16,2,16,1024]{3,2,0,1:T(8,128)(2,1)S(1)} all-to-all(bf16[16,2,16,1024]{3,2,0,1:T(8,128)(2,1)S(1)} %copy.13), channel_id=1, replica_groups=mesh['grp'=4,'blk_0'=4,'blk_1'=4,'blk_2'=2] {'blk_2'}, dimensions={1} | all-to-all | bytes 2097152 | tf_op jit(solution)/shard_map/all_to_all | solution.py:35
  47.2 1.0 copy-done.4
  48.2 1.1 copy.14
  49.3 2.5 %multiply_reduce_fusion = f32[]{:T(128)} fusion(bf16[16,2,16,1024]{3,2,0,1:T(8,128)(2,1)} %copy-done.4), kind=kLoop, calls=%fused_computation.13 | loop fusion | flops 1572863 | bytes 1048580 | tf_op jit(solution)/shard_map/reduce_sum | solution.py:112
  51.7 11.1 %psum.28 = f32[]{:T(128)} all-reduce(f32[]{:T(128)} %multiply_reduce_fusion), channel_id=1, replica_groups=mesh['grp'=4,'blk_0'=4,'blk_1'=4,'blk_2'=2] {'grp'}, use_global_device_ids=true, to_apply=%region_1.0 | all-reduce | flops 1 | bytes 8 | tf_op jit(solution)/shard_map/psum | solution.py:47
  62.8 9.2 %psum.29 = f32[]{:T(128)} all-reduce(f32[]{:T(128)} %psum.28), channel_id=1, replica_groups=mesh['grp'=4,'blk_0'=4,'blk_1'=4,'blk_2'=2] {'blk_0'}, use_global_device_ids=true, to_apply=%region_2.0 | all-reduce | flops 1 | bytes 8 | tf_op jit(solution)/shard_map/psum | solution.py:47
  72.0 9.2 %psum.30 = f32[]{:T(128)} all-reduce(f32[]{:T(128)} %psum.29), channel_id=1, replica_groups=mesh['grp'=4,'blk_0'=4,'blk_1'=4,'blk_2'=2] {'blk_1'}, use_global_device_ids=true, to_apply=%region_3.0 | all-reduce | flops 1 | bytes 8 | tf_op jit(solution)/shard_map/psum | solution.py:47
  81.2 3.1 %psum.31 = f32[]{:T(128)} all-reduce(f32[]{:T(128)} %psum.30), channel_id=1, replica_groups=mesh['grp'=4,'blk_0'=4,'blk_1'=4,'blk_2'=2] {'blk_2'}, use_global_device_ids=true, to_apply=%region_4.0 | all-reduce | flops 1 | bytes 8 | tf_op jit(solution)/shard_map/psum | solution.py:47
  84.3 1.3 copy.16
  86.3 8.9 %all-gather.2.cloned.1.call-done = bf16[2048,1024]{1,0:T(8,128)(2,1)} async-done(((bf16[512,1024]{1,0:T(8,128)(2,1)}), bf16[2048,1024]{1,0:T(8,128)(2,1)}) %all-gather.2.cloned.1.call-update) | async-done | bytes 4194320 | tf_op jit(solution)/shard_map/all_gather | solution.py:113
  95.2 7.8 %fusion.23 = f32[1024,1024]{1,0:T(8,128)S(1)} fusion(bf16[2048,1024]{1,0:T(8,128)(2,1)} %all-gather.2.cloned.1.call-done), kind=kOutput, calls=%fused_computation.37 | convolution fusion | flops 4294967296 | bytes 8388608 | tf_op jit(solution)/shard_map/dot_general | solution.py:93
  103.0 3.6 %fusion.20 = f32[1,1024]{1,0:T(1,128)S(1)} fusion(f32[1024,1024]{1,0:T(8,128)S(1)} %fusion.23), kind=kOutput, calls=%fused_computation.32 | convolution fusion | flops 12582912 | bytes 4198400 | tf_op jit(solution)/shard_map/dot_general | solution.py:62
  106.6 4.8 %fusion.26 = f32[1024,512]{1,0:T(8,128)} fusion(f32[1024,1024]{1,0:T(8,128)S(1)} %fusion.23, bf16[512,1024]{1,0:T(8,128)(2,1)S(1)} %bitcast.82), kind=kOutput, calls=%fused_computation.40 | convolution fusion | flops 6442450944 | bytes 7340032 | tf_op jit(solution)/shard_map/dot_general | solution.py:73
  111.4 0.6 multiply_reduce_fusion.3
  112.7 5.8 %fusion.24 = f32[1,1024]{1,0:T(1,128)S(1)} fusion(f32[1024,1024]{1,0:T(8,128)} %copy-done.1, f32[1024,1]{0,1:T(1,128)S(1)} %bitcast.91), kind=kOutput, calls=%fused_computation.38 | convolution fusion | flops 12582912 | bytes 4202496 | tf_op jit(solution)/shard_map/dot_general | solution.py:62
  118.4 0.6 multiply_reduce_fusion.2
  119.8 6.0 %fusion.25 = f32[1,1024]{1,0:T(1,128)S(1)} fusion(f32[1024,1024]{1,0:T(8,128)} %copy-done.1, f32[1024,1]{0,1:T(1,128)S(1)} %bitcast.92), kind=kOutput, calls=%fused_computation.39 | convolution fusion | flops 12582912 | bytes 4202496 | tf_op jit(solution)/shard_map/dot_general | solution.py:62
  125.7 0.6 multiply_reduce_fusion.1
  127.2 9.5 %fusion.8 = f32[1024,512]{1,0:T(8,128)S(1)} fusion(f32[1024,1024]{1,0:T(8,128)} %copy-done.1, bf16[512,1024]{0,1:T(8,128)(2,1)} %copy.16, f32[1024,512]{1,0:T(8,128)} %fusion.26, f32[]{:T(128)S(6)} %mul.111, f32[]{:T(128)S(6)} %div.36, f32[]{:T(128)S(6)} %div.41), kind=kOutput, calls=%fused_computation.15 | convolution fusion | flops 6446120960 | bytes 9437196 | tf_op jit(solution)/shard_map/dot_general | solution.py:73
  136.8 9.6 %fusion.11 = bf16[1024,512,1]{1,0,2:T(8,128)(2,1)S(1)} fusion(f32[1024,1024]{1,0:T(8,128)S(1)} %copy-done.2, f32[1024,512]{1,0:T(8,128)S(1)} %fusion.8, bf16[512,1024]{0,1:T(8,128)(2,1)S(1)} %copy-done.6, f32[1024,512]{1,0:T(8,128)S(1)} %copy-done.5, f32[]{:T(128)S(6)} %integer_pow.11, f32[]{:T(128)S(6)} %div.47, f32[]{:T(128)S(6)} %integer_pow.10, ...), kind=kOutput, calls=%fused_computation.17 | convolution fusion | flops 6463422464 | bytes 10485792 | tf_op jit(solution)/shard_map/dot_general | solution.py:73
  146.4 0.7 fusion.27
  147.1 24.3 %all_to_all.17 = f32[32,16,512]{2,1,0:T(8,128)S(1)} all-to-all(f32[32,16,512]{2,1,0:T(8,128)S(1)} %fusion.27), channel_id=1, replica_groups=mesh['grp'=4,'blk_0'=4,'blk_1'=4,'blk_2'=2] {'blk_0','blk_1','blk_2'}, dimensions={0} | all-to-all | bytes 2097152 | tf_op jit(solution)/shard_map/all_to_all | solution.py:53
  171.4 0.1 reduce_sum.49
  171.5 0.6 broadcast_multiply_fusion
  (18 shorter events, 0.1 us)
Async XLA Ops:
  6.5 4.9 %copy-start = (bf16[3072,256]{1,0:T(8,128)(2,1)S(1)}, bf16[3072,256]{1,0:T(8,128)(2,1)}, u32[]{:S(2)}) copy-start(bf16[3072,256]{1,0:T(8,128)(2,1)} %param.7) | copy-start | bytes 4718596
  6.5 88.7 %all-gather.2.cloned.1.call-start = ((), (), s32[]{:S(2)}) async-start(), calls=%async_computation.3 | async-start | bytes 5242880 | tf_op jit(solution)/shard_map/all_gather | solution.py:113
  6.5 5.3 %copy-start.7 = (bf16[1024,3072]{1,0:T(8,128)(2,1)S(1)}, bf16[1024,3072]{1,0:T(8,128)(2,1)}, u32[]{:S(2)}) copy-start(bf16[1024,3072]{1,0:T(8,128)(2,1)} %param.5) | copy-start | bytes 18874372
  47.2 1.0 copy-start.4
  49.2 35.1 %copy-start.3 = (bf16[16,2,16,1024]{3,2,1,0:T(8,128)(2,1)S(1)}, bf16[16,2,16,1024]{3,2,1,0:T(8,128)(2,1)}, u32[]{:S(2)}) copy-start(bf16[16,2,16,1024]{3,2,1,0:T(8,128)(2,1)} %copy.14) | copy-start | bytes 3145732
  103.0 3.6 %copy-start.1 = (f32[1024,1024]{1,0:T(8,128)}, f32[1024,1024]{1,0:T(8,128)S(1)}, u32[]{:S(2)}) copy-start(f32[1024,1024]{1,0:T(8,128)S(1)} %fusion.23) | copy-start | bytes 12582916
  127.2 9.6 %copy-start.2 = (f32[1024,1024]{1,0:T(8,128)S(1)}, f32[1024,1024]{1,0:T(8,128)}, u32[]{:S(2)}) copy-start(f32[1024,1024]{1,0:T(8,128)} %copy-done.1) | copy-start | bytes 12582916
  127.2 9.6 %copy-start.5 = (f32[1024,512]{1,0:T(8,128)S(1)}, f32[1024,512]{1,0:T(8,128)}, u32[]{:S(2)}) copy-start(f32[1024,512]{1,0:T(8,128)} %fusion.26) | copy-start | bytes 6291460
  127.2 9.6 %copy-start.6 = (bf16[512,1024]{0,1:T(8,128)(2,1)S(1)}, bf16[512,1024]{0,1:T(8,128)(2,1)}, u32[]{:S(2)}) copy-start(bf16[512,1024]{0,1:T(8,128)(2,1)} %copy.16) | copy-start | bytes 3145732
Sparse Core Ops, SparseCore 0:
  49.4 45.7 all-gather.1
where the time goes:
time: 180 us; the launch traced here: 179 us
  blocking collectives  86.6 us (48%)
  matrix products  54.8 us (30%)
  between operations  16.4 us (9%)
  waiting for transfers between devices  8.9 us (5%)
  local copies, waits for them, and re-layouts  7.22 us (4%)
  other arithmetic  4.99 us (3%)
    psum x4, blocking collectives, one_axis_at_a_time(): array = lax.psum(array, axis)  32.6 us
    all_to_all x2, blocking collectives, moved_by_axis(): lax.all_to_all(blocks, axes[k], split_axis=k, concat_axis=k, tiled=True)  29.7 us
    all_to_all x1, blocking collectives, sum_at_owner(): blocks = lax.all_to_all(split_up(array, dim, size), axis, 0, 0, tiled=True)  24.3 us
    dot_general x3, matrix products, operate(): jnp.dot(gram_sum, field, precision=lax.Precision.HIGHEST) + damping * field  23.9 us
    dot_general x3, matrix products, top_estimate(): image = jnp.dot(gram_sum, vector, precision=lax.Precision.HIGHEST)  15.3 us
    all_gather x1, waiting for transfers between devices, shards(): lax.all_gather(block_rows, 'grp', axis=0, tiled=True)  8.88 us
    dot_general x1, matrix products, self_product(): lax.dot_general(rows, rows, (((0,), (0,)), ((), ())), preferred_element_t...  7.76 us
    dot_general x1, matrix products, shards(): jnp.dot(activations, proj_act, preferred_element_type=jnp.float32)  4.87 us
  transfers between devices with their start and end apart: 1, of which 1 were waited for; matrix products, arithmetic and copies ran while one was open for 2% of the time, Pallas kernels for 0%

commit v1 on v0

v1 whole, which is shorter than its diff:
```python
import functools

import jax
import jax.numpy as jnp
from jax import lax
from jax.experimental import pallas as pl
from jax.experimental.pallas import tpu as pltpu
from jax.sharding import Mesh
from jax.sharding import PartitionSpec as P

SEQ = 64
ITERS = 4
BLK = ("blk_0", "blk_1", "blk_2")
GRP_BLK = ("grp", "blk_0", "blk_1", "blk_2")
TILE = 128
PIECES = 9

damping_rate = 0.5
power_steps = 3


def mxu(a, b, dims):
    return lax.dot_general(a, b, (dims, ((), ())), preferred_element_type=jnp.float32)


def feature_kernel(
    act_ref, grad_ref, pa_ref, po_ref, out_ref, sum_ref, act_low, grad_low, feats, by_coord
):
    step = pl.program_id(0)
    steps = pl.num_programs(0)
    tokens = act_ref.shape[0]
    rows = pl.ds(pl.multiple_of(step * tokens, tokens), tokens)
    act_low[rows, :] = mxu(act_ref[...], pa_ref[...], ((1,), (0,))).astype(jnp.bfloat16)
    grad_low[rows, :] = mxu(grad_ref[...], po_ref[...], ((1,), (0,))).astype(jnp.bfloat16)
    blocks, examples, width = out_ref.shape
    per = width // grad_low.shape[1]
    cols = grad_low.shape[1]

    def eight(half):
        for e in range(8):
            at = pl.ds((half * 8 + e) * SEQ, SEQ)
            feats[e] = mxu(act_low[at, :], grad_low[at, :], ((0,), (0,)))
        turned = jnp.swapaxes(feats[...], 0, 1)
        turned = turned.reshape(blocks, per, 8, cols)
        for j in range(per):
            by_coord[:, half * 8 : half * 8 + 8, j * cols : (j + 1) * cols] = turned[:, j]

    @pl.when(step == steps // 2)
    def _():
        eight(0)

    @pl.when(step == steps - 1)
    def _():
        eight(1)
        acc = jnp.zeros((examples, width), jnp.float32)
        for k in range(blocks):
            low = by_coord[k].astype(jnp.bfloat16)
            out_ref[k] = low
            wide = low.astype(jnp.float32)
            acc = acc + wide * wide
        part = jnp.zeros((8, TILE), jnp.float32)
        for r in range(0, examples, 8):
            for c in range(0, width, TILE):
                part = part + acc[r : r + 8, c : c + TILE]
        sum_ref[...] = part


def features_of(activations, out_grads, proj_act, proj_out, blocks):
    arguments = (activations, out_grads, proj_act, proj_out)
    tokens, depth = activations.shape
    examples = tokens // SEQ
    ra, rb = proj_act.shape[1], proj_out.shape[1]
    width = ra * rb // blocks
    steps = 4
    size = tokens // steps
    return pl.pallas_call(
        feature_kernel,
        grid=(steps,),
        in_specs=[
            pl.BlockSpec((size, depth), lambda i: (i, 0)),
            pl.BlockSpec((size, depth), lambda i: (i, 0)),
            pl.BlockSpec((depth, ra), lambda i: (0, 0), pipeline_mode=pl.Buffered(1)),
            pl.BlockSpec((depth, rb), lambda i: (0, 0), pipeline_mode=pl.Buffered(1)),
        ],
        out_specs=[
            pl.BlockSpec((blocks, examples, width), lambda i: (0, 0, 0)),
            pl.BlockSpec((8, TILE), lambda i: (0, 0)),
        ],
        out_shape=[
            jax.ShapeDtypeStruct((blocks, examples, width), jnp.bfloat16),
            jax.ShapeDtypeStruct((8, TILE), jnp.float32),
        ],
        scratch_shapes=[
            pltpu.VMEM((tokens, ra), jnp.bfloat16),
            pltpu.VMEM((tokens, rb), jnp.bfloat16),
            pltpu.VMEM((8, ra, rb), jnp.float32),
            pltpu.VMEM((blocks, examples, width), jnp.float32),
        ],
        compiler_params=pltpu.CompilerParams(
            dimension_semantics=("arbitrary",), vmem_limit_bytes=32 << 20
        ),
        name="features",
    )(*(pltpu.with_memory_space_constraint(x, pltpu.HBM) for x in arguments))


def places(high):
    return (
        (0, 0),
        (0, 1),
        (1, 1),
        (0, 2),
        (0, 3),
        (1, 2),
        (1, 3),
        (0, 5),
        (high, high + 4),
    )


def gram_kernel(place_ref, rows_ref, own_ref, up_ref, two_ref, down_ref, parts):
    wide = 2 * TILE

    def columns(first, count):
        return rows_ref[:, first * TILE : (first + count) * TILE]

    for q in range(4):
        left = columns(2 * q, 2)
        near = mxu(left, columns(2 * q, 2), ((0,), (0,)))
        after = mxu(left, columns((2 * q + 2) % 8, 2), ((0,), (0,)))
        if q < 2:
            far = mxu(columns(2 * q, 1), columns(2 * q + 4, 2), ((0,), (0,)))
            last = (far[:, TILE:wide], far[:, :TILE])
        else:
            far = mxu(left, columns((2 * q + 5) % 8, 1), ((0,), (0,)))
            last = (far[:TILE], far[TILE:wide])
        pieces = (
            near[:TILE, :TILE],
            near[:TILE, TILE:],
            near[TILE:, TILE:],
            after[:TILE, :TILE],
            after[:TILE, TILE:],
            after[TILE:, :TILE],
            after[TILE:, TILE:],
        ) + last
        for n, piece in enumerate(pieces):
            parts[q, n] = piece
    place = place_ref[0]
    own_ref[...] = parts[place]
    for shift, ref in ((1, up_ref), (2, two_ref), (3, down_ref)):
        ref[...] = parts[lax.rem(place + shift, 4)].astype(jnp.bfloat16)


def gram_parts(place, rows):
    shape = (PIECES, TILE, TILE)
    return pl.pallas_call(
        gram_kernel,
        in_specs=[
            pl.BlockSpec(memory_space=pltpu.SMEM),
            pl.BlockSpec(memory_space=pltpu.VMEM),
        ],
        out_specs=[pl.BlockSpec(memory_space=pltpu.VMEM)] * 4,
        out_shape=[jax.ShapeDtypeStruct(shape, jnp.float32)]
        + [jax.ShapeDtypeStruct(shape, jnp.bfloat16)] * 3,
        scratch_shapes=[pltpu.VMEM((4,) + shape, jnp.float32)],
        compiler_params=pltpu.CompilerParams(vmem_limit_bytes=16 << 20),
        name="gram_parts",
    )(place, rows)


def solve_kernel(place_ref, total_ref, own_ref, one_ref, two_ref, three_ref, rows_ref, out_ref, gram):
    place = place_ref[0]
    for back, ref in ((0, own_ref), (1, one_ref), (2, two_ref), (3, three_ref)):
        quarter = lax.rem(place + 4 - back, 4)
        high = lax.div(quarter, 2)
        for n, (i, j) in enumerate(places(high)):
            piece = ref[n]
            row = pl.multiple_of(lax.rem(2 * quarter + i, 8) * TILE, TILE)
            col = pl.multiple_of(lax.rem(2 * quarter + j, 8) * TILE, TILE)
            gram[pl.ds(row, TILE), pl.ds(col, TILE)] = piece
            if n not in (0, 2):
                gram[pl.ds(col, TILE), pl.ds(row, TILE)] = piece.T
    width = gram.shape[0]
    turn = lax.broadcasted_iota(jnp.int32, (16, width), 0)
    vector = jnp.full((1, width), 1.0 / width**0.5, jnp.float32)
    for _ in range(power_steps):
        high = vector.astype(jnp.bfloat16).astype(jnp.float32)
        rest = vector - high
        mid = rest.astype(jnp.bfloat16).astype(jnp.float32)
        low = rest - mid
        three = jnp.where(turn == 0, high, jnp.where(turn == 1, mid, jnp.where(turn == 2, low, 0.0)))
        image = mxu(three.astype(jnp.bfloat16), gram[...], ((1,), (0,)))
        image = jnp.sum(image, axis=0, keepdims=True)
        radius = jnp.sqrt(jnp.sum(image * image, axis=1, keepdims=True) + 1e-06)
        vector = image / radius
    damping = total_ref[0] * damping_rate
    center = damping + radius

    rows = rows_ref[...]
    right_side = rows.astype(jnp.float32)

    def operate(field):
        return mxu(field.astype(jnp.bfloat16), gram[...], ((1,), (0,))) + damping * field

    stride = 1.0 / center
    direction = right_side
    solution = stride * direction
    residual = right_side - stride * operate(direction)
    for sweep in range(1, ITERS):
        if sweep == 1:
            momentum = 0.5 * (radius * stride) ** 2
        else:
            momentum = (0.5 * radius * stride) ** 2
        stride = 1.0 / (center - momentum / stride)
        direction = residual + momentum * direction
        solution = solution + stride * direction
        if sweep + 1 < ITERS:
            residual = residual - stride * operate(direction)
    out_ref[...] = mxu(rows, solution.astype(jnp.bfloat16), ((1,), (1,))).astype(out_ref.dtype)


def block_scores(place, mean_square, quarters, rows):
    vmem = pl.BlockSpec(memory_space=pltpu.VMEM)
    smem = pl.BlockSpec(memory_space=pltpu.SMEM)
    examples, width = rows.shape
    return pl.pallas_call(
        solve_kernel,
        in_specs=[smem, smem, vmem, vmem, vmem, vmem, vmem],
        out_specs=vmem,
        out_shape=jax.ShapeDtypeStruct((examples, examples), jnp.bfloat16),
        scratch_shapes=[pltpu.VMEM((width, width), jnp.bfloat16)],
        compiler_params=pltpu.CompilerParams(vmem_limit_bytes=32 << 20),
        name="solve",
    )(place, mean_square, *quarters, rows)


def shifted(value, axis, shift):
    size = lax.axis_size(axis)
    return lax.ppermute(value, axis, [(i, (i + shift) % size) for i in range(size)])


def sum_over(value, axis):
    size = lax.axis_size(axis)
    shift = 1
    while shift < size:
        value = value + shifted(value, axis, shift)
        shift *= 2
    return value


def shards(activations, out_grads, proj_act, proj_out):
    examples = activations.shape[0] // SEQ
    blocks = lax.axis_size(BLK)
    by_block, squares = features_of(activations, out_grads, proj_act, proj_out, blocks)
    arrived = lax.all_to_all(by_block, BLK, 0, 0, tiled=True)
    rows = arrived.reshape(blocks * examples, -1)
    width = rows.shape[1]

    total = squares
    for axis in ("grp", "blk_2"):
        total = sum_over(total, axis)
    rows, total = lax.optimization_barrier((rows, total))

    place = lax.axis_index("grp").astype(jnp.int32).reshape(1)
    own, up, two, down = gram_parts(place, rows)
    others = [shifted(part, "grp", shift) for shift, part in ((1, up), (2, two), (3, down))]
    total = sum_over(total, "blk_1")
    total, *others = lax.optimization_barrier((total, *others))
    quarter = own
    for part in others:
        quarter = quarter + part.astype(jnp.float32)
    quarter = quarter.astype(jnp.bfloat16)
    quarters = [quarter] + [shifted(quarter, "grp", shift) for shift in (1, 2, 3)]
    total = sum_over(total, "blk_0")
    mean_square = (jnp.sum(total) / (width * blocks)).reshape(1)
    term = block_scores(place, mean_square, quarters, rows)
    terms = lax.all_to_all(term.reshape(blocks, examples, -1), BLK, 0, 0, tiled=True)
    scores = jnp.sum(terms.astype(jnp.float32), axis=0)
    return scores * float(examples * lax.axis_size("grp"))


def solution(mesh):
    split = Mesh(
        mesh.devices.reshape(mesh.shape["grp"], 4, 4, 2), ("grp", "blk_0", "blk_1", "blk_2")
    )
    placed = (P(GRP_BLK, None), P(GRP_BLK, None), P(), P())
    return jax.shard_map(
        shards, mesh=split, in_specs=placed, out_specs=P(GRP_BLK, None), check_vma=False
    )
```

time: 180 us -> 96.9 us (0.54)
  blocking collectives: 86.6 us -> 15.6 us
  matrix products: 54.8 us -> 0 us
  waiting for transfers between devices: 8.9 us -> 38.2 us
  starting transfers between devices: 0.01 us -> 22.4 us
  Pallas kernels: 0 us -> 17.2 us
  between operations: 16.4 us -> 0.69 us
  local copies, waits for them, and re-layouts: 7.22 us -> 0 us
  other arithmetic: 4.99 us -> 1.54 us
    dot_general x11 -> x0, matrix products: 54.8 us -> none  [the longest x3 23.9 us: operate(): jnp.dot(gram_sum, field, precision=lax.Precision.HIGHEST) + damping * field]
    all_to_all x3 -> x1, blocking collectives: 54 us -> 15.6 us  [shards(): lax.all_to_all(term.reshape(blocks, examples, -1), BLK, 0, 0, tiled=True)]
    psum x4 -> x0, blocking collectives: 32.6 us -> none  [one_axis_at_a_time(): array = lax.psum(array, axis)]
    ppermute x0 -> x13, waiting for transfers between devices: none -> 32.1 us  [shifted(): lax.ppermute(value, axis, [(i, (i + shift) % size) for i in range(size)])]
    pallas_call x0 -> x3, Pallas kernels: none -> 17.2 us  [the longest x1 9.48 us: features_of(): pl.pallas_call(feature_kernel, grid=(steps,), in_specs=[pl.BlockSpec((siz...]
    ppermute x0 -> x13, starting transfers between devices: none -> 14 us  [shifted(): lax.ppermute(value, axis, [(i, (i + shift) % size) for i in range(size)])]
    all_gather x1 -> x0, waiting for transfers between devices: 8.88 us -> none  [shards(): lax.all_gather(block_rows, 'grp', axis=0, tiled=True)]
    all_to_all x0 -> x1, starting transfers between devices: none -> 8.42 us  [shards(): arrived = lax.all_to_all(by_block, BLK, 0, 0, tiled=True)]
  transfers between devices with their start and end apart: 1 -> 14, of which waited for: 1 -> 10; matrix products, arithmetic and copies ran while one was open for 2% -> 1% of each run, Pallas kernels for 0% -> 0%
where the time goes in v1:
time: 96.9 us; the launch traced here: 95.7 us
  waiting for transfers between devices  38.2 us (39%)
  starting transfers between devices  22.4 us (23%)
  Pallas kernels  17.2 us (18%)
  blocking collectives  15.6 us (16%)
  other arithmetic  1.54 us (2%)
    ppermute x13, waiting for transfers between devices, shifted(): lax.ppermute(value, axis, [(i, (i + shift) % size) for i in range(size)])  32.1 us
    all_to_all x1, blocking collectives, shards(): lax.all_to_all(term.reshape(blocks, examples, -1), BLK, 0, 0, tiled=True)  15.6 us
    ppermute x13, starting transfers between devices, shifted(): lax.ppermute(value, axis, [(i, (i + shift) % size) for i in range(size)])  14 us
    pallas_call x1, Pallas kernels, features_of(): pl.pallas_call(feature_kernel, grid=(steps,), in_specs=[pl.BlockSpec((siz...  9.48 us
    all_to_all x1, starting transfers between devices, shards(): arrived = lax.all_to_all(by_block, BLK, 0, 0, tiled=True)  8.42 us
    pallas_call x1, Pallas kernels, block_scores(): pl.pallas_call(solve_kernel, in_specs=[smem, smem, vmem, vmem, vmem, vmem...  6.57 us
    all_to_all x1, waiting for transfers between devices, shards(): arrived = lax.all_to_all(by_block, BLK, 0, 0, tiled=True)  6.16 us
  transfers between devices with their start and end apart: 14, of which 10 were waited for; matrix products, arithmetic and copies ran while one was open for 1% of the time, Pallas kernels for 0%

profile of v1, /device:TPU:0, one launch (start us, length us, event | category | flops | bytes accessed | tf_op | source)
XLA Modules:
  0.0 95.7 jit_solution(15426309369182912006)
XLA Ops:
  0.0 9.5 %features.1 = (bf16[32,16,1024]{2,1,0:T(8,128)(2,1)}, f32[8,128]{1,0:T(8,128)S(1)}) custom-call(bf16[1024,3072]{1,0:T(8,128)(2,1)} %act_ref.1, bf16[1024,3072]{1,0:T(8,128)(2,1)} %grad_ref.1, bf16[3072,128]{1,0:T(8,128)(2,1)} %pa_ref.1, bf16[3072,256]{1,0:T(8,128)(2,1)} %po_ref.1), custom_call_target="tpu_custom_call" | custom-call | tf_op jit(solution)/shard_map/features/pallas_call | solution.py:76
  9.5 8.4 %all-to-all-start = ((bf16[32,16,1024]{2,1,0:T(8,128)(2,1)}), bf16[32,16,1024]{2,1,0:T(8,128)(2,1)S(1)}, u32[]{:S(2)}, u32[]{:S(2)}) async-start(bf16[32,16,1024]{2,1,0:T(8,128)(2,1)} %get-tuple-element.17), calls=%async_computation | async-start | bytes 2097152 | tf_op jit(solution)/shard_map/all_to_all | solution.py:254
  17.9 1.6 %collective-permute-start = (f32[8,128]{1,0:T(8,128)S(1)}, f32[8,128]{1,0:T(8,128)S(1)}, u32[]{:S(2)}, u32[]{:S(2)}) collective-permute-start(f32[8,128]{1,0:T(8,128)S(1)} %get-tuple-element.18), channel_id=1, source_target_pairs={{0,32},{32,64},{64,96},{96,0},{1,33},{33,65},{65,97},{97,1},{2,34}... | collective-permute-start | bytes 12296 | tf_op jit(solution)/shard_map/ppermute | solution.py:238
  19.5 3.3 %collective-permute-done = f32[8,128]{1,0:T(8,128)S(1)} collective-permute-done((f32[8,128]{1,0:T(8,128)S(1)}, f32[8,128]{1,0:T(8,128)S(1)}, u32[]{:S(2)}, u32[]{:S(2)}) %collective-permute-start) | collective-permute-done | bytes 4128 | tf_op jit(solution)/shard_map/ppermute | solution.py:238
  22.8 1.8 %collective-permute-start.1 = (f32[8,128]{1,0:T(8,128)S(1)}, f32[8,128]{1,0:T(8,128)S(1)}, u32[]{:S(2)}, u32[]{:S(2)}) collective-permute-start(f32[8,128]{1,0:T(8,128)S(1)} %add.30), channel_id=1, source_target_pairs={{0,64},{32,96},{64,0},{96,32},{1,65},{33,97},{65,1},{97,33},{2,66}... | collective-permute-start | bytes 12296 | tf_op jit(solution)/shard_map/ppermute | solution.py:238
  24.6 3.3 %collective-permute-done.1 = f32[8,128]{1,0:T(8,128)S(1)} collective-permute-done((f32[8,128]{1,0:T(8,128)S(1)}, f32[8,128]{1,0:T(8,128)S(1)}, u32[]{:S(2)}, u32[]{:S(2)}) %collective-permute-start.1) | collective-permute-done | bytes 4128 | tf_op jit(solution)/shard_map/ppermute | solution.py:238
  27.9 0.0 collective-permute-start.2
  27.9 1.2 %collective-permute-done.2 = f32[8,128]{1,0:T(8,128)S(1)} collective-permute-done((f32[8,128]{1,0:T(8,128)S(1)}, f32[8,128]{1,0:T(8,128)S(1)}, u32[]{:S(2)}, u32[]{:S(2)}) %collective-permute-start.2) | collective-permute-done | bytes 4128 | tf_op jit(solution)/shard_map/ppermute | solution.py:238
  29.1 6.2 %all-to-all-done = bf16[32,16,1024]{2,1,0:T(8,128)(2,1)S(1)} async-done(((bf16[32,16,1024]{2,1,0:T(8,128)(2,1)}), bf16[32,16,1024]{2,1,0:T(8,128)(2,1)S(1)}, u32[]{:S(2)}, u32[]{:S(2)}) %all-to-all-start) | async-done | bytes 1048608 | tf_op jit(solution)/shard_map/all_to_all | solution.py:254
  35.2 1.2 %gram_parts.1 = (f32[9,128,128]{2,1,0:T(8,128)S(1)}, bf16[9,128,128]{2,1,0:T(8,128)(2,1)S(1)}, bf16[9,128,128]{2,1,0:T(8,128)(2,1)S(1)}, bf16[9,128,128]{2,1,0:T(8,128)(2,1)S(1)}) custom-call(s32[1]{0:T(128)} %bitcast.place_ref, bf16[512,1024]{1,0:T(8,128)(2,1)S(1)} %bitcast.4), custom_call_target="tpu_custom_call" | custom-call | tf_op jit(solution)/shard_map/gram_parts/pallas_call | solution.py:155
  36.4 1.6 %collective-permute-start.5 = (bf16[9,128,128]{2,1,0:T(8,128)(2,1)S(1)}, bf16[9,128,128]{2,1,0:T(8,128)(2,1)S(1)}, u32[]{:S(2)}, u32[]{:S(2)}) collective-permute-start(bf16[9,128,128]{2,1,0:T(8,128)(2,1)S(1)} %get-tuple-element.21), channel_id=1, source_target_pairs={{0,32},{32,64},{64,96},{96,0},{1,33},{33,65},{65,97},{97,1},{2,34}... | collective-permute-start | bytes 884744 | tf_op jit(solution)/shard_map/ppermute | solution.py:238
  38.0 2.7 %collective-permute-start.6 = (bf16[9,128,128]{2,1,0:T(8,128)(2,1)S(1)}, bf16[9,128,128]{2,1,0:T(8,128)(2,1)S(1)}, u32[]{:S(2)}, u32[]{:S(2)}) collective-permute-start(bf16[9,128,128]{2,1,0:T(8,128)(2,1)S(1)} %get-tuple-element.22), channel_id=1, source_target_pairs={{0,64},{32,96},{64,0},{96,32},{1,65},{33,97},{65,1},{97,33},{2,66}... | collective-permute-start | bytes 884744 | tf_op jit(solution)/shard_map/ppermute | solution.py:238
  40.7 1.5 %collective-permute-start.7 = (bf16[9,128,128]{2,1,0:T(8,128)(2,1)S(1)}, bf16[9,128,128]{2,1,0:T(8,128)(2,1)S(1)}, u32[]{:S(2)}, u32[]{:S(2)}) collective-permute-start(bf16[9,128,128]{2,1,0:T(8,128)(2,1)S(1)} %get-tuple-element.23), channel_id=1, source_target_pairs={{0,96},{32,0},{64,32},{96,64},{1,97},{33,1},{65,33},{97,65},{2,98}... | collective-permute-start | bytes 884744 | tf_op jit(solution)/shard_map/ppermute | solution.py:238
  42.1 0.6 collective-permute-start.3
  42.7 4.2 %collective-permute-done.3 = f32[8,128]{1,0:T(8,128)S(1)} collective-permute-done((f32[8,128]{1,0:T(8,128)S(1)}, f32[8,128]{1,0:T(8,128)S(1)}, u32[]{:S(2)}, u32[]{:S(2)}) %collective-permute-start.3) | collective-permute-done | bytes 4128 | tf_op jit(solution)/shard_map/ppermute | solution.py:238
  47.0 0.1 collective-permute-start.4
  47.0 5.1 %collective-permute-done.4 = f32[8,128]{1,0:T(8,128)S(1)} collective-permute-done((f32[8,128]{1,0:T(8,128)S(1)}, f32[8,128]{1,0:T(8,128)S(1)}, u32[]{:S(2)}, u32[]{:S(2)}) %collective-permute-start.4) | collective-permute-done | bytes 4128 | tf_op jit(solution)/shard_map/ppermute | solution.py:238
  52.1 1.9 %collective-permute-done.6 = bf16[9,128,128]{2,1,0:T(8,128)(2,1)S(1)} collective-permute-done((bf16[9,128,128]{2,1,0:T(8,128)(2,1)S(1)}, bf16[9,128,128]{2,1,0:T(8,128)(2,1)S(1)}, u32[]{:S(2)}, u32[]{:S(2)}) %collective-permute-start.6) | collective-permute-done | bytes 294944 | tf_op jit(solution)/shard_map/ppermute | solution.py:238
  54.0 0.2 add_convert_fusion.own_ref
  54.2 2.3 %collective-permute-start.12 = (bf16[9,128,128]{2,1,0:T(8,128)(2,1)S(1)}, bf16[9,128,128]{2,1,0:T(8,128)(2,1)S(1)}, u32[]{:S(2)}, u32[]{:S(2)}) collective-permute-start(bf16[9,128,128]{2,1,0:T(8,128)(2,1)S(1)} %add_convert_fusion.own_ref), channel_id=1, source_target_pairs={{0,96},{32,0},{64,32},{96,64},{1,97},{33,1},{65,33},{97,65},{2,98}... | collective-permute-start | bytes 884744 | tf_op jit(solution)/shard_map/ppermute | solution.py:238
  56.5 1.1 %collective-permute-start.11 = (bf16[9,128,128]{2,1,0:T(8,128)(2,1)S(1)}, bf16[9,128,128]{2,1,0:T(8,128)(2,1)S(1)}, u32[]{:S(2)}, u32[]{:S(2)}) collective-permute-start(bf16[9,128,128]{2,1,0:T(8,128)(2,1)S(1)} %add_convert_fusion.own_ref), channel_id=1, source_target_pairs={{0,64},{32,96},{64,0},{96,32},{1,65},{33,97},{65,1},{97,33},{2,66}... | collective-permute-start | bytes 884744 | tf_op jit(solution)/shard_map/ppermute | solution.py:238
  57.7 0.7 collective-permute-start.10
  58.3 0.0 collective-permute-start.8
  58.4 4.8 %collective-permute-done.8 = f32[8,128]{1,0:T(8,128)S(1)} collective-permute-done((f32[8,128]{1,0:T(8,128)S(1)}, f32[8,128]{1,0:T(8,128)S(1)}, u32[]{:S(2)}, u32[]{:S(2)}) %collective-permute-start.8) | collective-permute-done | bytes 4128 | tf_op jit(solution)/shard_map/ppermute | solution.py:238
  63.2 0.1 collective-permute-start.9
  63.3 5.0 %collective-permute-done.9 = f32[8,128]{1,0:T(8,128)S(1)} collective-permute-done((f32[8,128]{1,0:T(8,128)S(1)}, f32[8,128]{1,0:T(8,128)S(1)}, u32[]{:S(2)}, u32[]{:S(2)}) %collective-permute-start.9) | collective-permute-done | bytes 4128 | tf_op jit(solution)/shard_map/ppermute | solution.py:238
  68.3 0.7 add_reduce_fusion
  69.6 3.2 %collective-permute-done.10.one_ref = bf16[9,128,128]{2,1,0:T(8,128)(2,1)S(1)} collective-permute-done((bf16[9,128,128]{2,1,0:T(8,128)(2,1)S(1)}, bf16[9,128,128]{2,1,0:T(8,128)(2,1)S(1)}, u32[]{:S(2)}, u32[]{:S(2)}) %collective-permute-start.10) | collective-permute-done | bytes 294944 | tf_op jit(solution)/shard_map/ppermute | solution.py:238
  72.8 6.6 %solve.1 = bf16[512,512]{1,0:T(8,128)(2,1)S(1)} custom-call(s32[1]{0:T(128)} %bitcast.place_ref, f32[1]{0:T(128)} %bitcast.2.total_ref, bf16[9,128,128]{2,1,0:T(8,128)(2,1)S(1)} %add_convert_fusion.own_ref, bf16[9,128,128]{2,1,0:T(8,128)(2,1)S(1)} %collective-permute-done.10.one_ref, bf16[9,128,128]{2,1,0:T(8,128)(2,1)S(1)} %collective-permute-done.11.two_ref, ...), custom_call_target="tpu_custom_call" | custom-call | tf_op jit(solution)/shard_map/solve/pallas_call | solution.py:225
  79.4 15.6 %all_to_all.10 = bf16[32,16,512]{2,1,0:T(8,128)(2,1)S(1)} all-to-all(bf16[32,16,512]{2,1,0:T(8,128)(2,1)S(1)} %bitcast.6), channel_id=1, replica_groups=mesh['grp'=4,'blk_0'=4,'blk_1'=4,'blk_2'=2] {'blk_0','blk_1','blk_2'}, dimensions={0} | all-to-all | bytes 1048576 | tf_op jit(solution)/shard_map/all_to_all | solution.py:276
  95.0 0.1 convert_reduce_fusion
  95.1 0.6 broadcast_multiply_fusion
  (10 shorter events, 0.0 us)
Async XLA Ops:
  9.5 25.8 %all-to-all-start = ((bf16[32,16,1024]{2,1,0:T(8,128)(2,1)}), bf16[32,16,1024]{2,1,0:T(8,128)(2,1)S(1)}, u32[]{:S(2)}, u32[]{:S(2)}) async-start(bf16[32,16,1024]{2,1,0:T(8,128)(2,1)} %get-tuple-element.17), calls=%async_computation | async-start | bytes 2097152 | tf_op jit(solution)/shard_map/all_to_all | solution.py:254
  17.9 4.9 %collective-permute-start = (f32[8,128]{1,0:T(8,128)S(1)}, f32[8,128]{1,0:T(8,128)S(1)}, u32[]{:S(2)}, u32[]{:S(2)}) collective-permute-start(f32[8,128]{1,0:T(8,128)S(1)} %get-tuple-element.18), channel_id=1, source_target_pairs={{0,32},{32,64},{64,96},{96,0},{1,33},{33,65},{65,97},{97,1},{2,34}... | collective-permute-start | bytes 12296 | tf_op jit(solution)/shard_map/ppermute | solution.py:238
  22.8 5.1 %collective-permute-start.1 = (f32[8,128]{1,0:T(8,128)S(1)}, f32[8,128]{1,0:T(8,128)S(1)}, u32[]{:S(2)}, u32[]{:S(2)}) collective-permute-start(f32[8,128]{1,0:T(8,128)S(1)} %add.30), channel_id=1, source_target_pairs={{0,64},{32,96},{64,0},{96,32},{1,65},{33,97},{65,1},{97,33},{2,66}... | collective-permute-start | bytes 12296 | tf_op jit(solution)/shard_map/ppermute | solution.py:238
  27.9 1.2 %collective-permute-start.2 = (f32[8,128]{1,0:T(8,128)S(1)}, f32[8,128]{1,0:T(8,128)S(1)}, u32[]{:S(2)}, u32[]{:S(2)}) collective-permute-start(f32[8,128]{1,0:T(8,128)S(1)} %add.31), channel_id=1, source_target_pairs={{0,1},{1,0},{2,3},{3,2},{4,5},{5,4},{6,7},{7,6},{8,9},{9,8},{10,11... | collective-permute-start | bytes 12296 | tf_op jit(solution)/shard_map/ppermute | solution.py:238
  36.4 15.7 %collective-permute-start.5 = (bf16[9,128,128]{2,1,0:T(8,128)(2,1)S(1)}, bf16[9,128,128]{2,1,0:T(8,128)(2,1)S(1)}, u32[]{:S(2)}, u32[]{:S(2)}) collective-permute-start(bf16[9,128,128]{2,1,0:T(8,128)(2,1)S(1)} %get-tuple-element.21), channel_id=1, source_target_pairs={{0,32},{32,64},{64,96},{96,0},{1,33},{33,65},{65,97},{97,1},{2,34}... | collective-permute-start | bytes 884744 | tf_op jit(solution)/shard_map/ppermute | solution.py:238
  38.0 16.0 %collective-permute-start.6 = (bf16[9,128,128]{2,1,0:T(8,128)(2,1)S(1)}, bf16[9,128,128]{2,1,0:T(8,128)(2,1)S(1)}, u32[]{:S(2)}, u32[]{:S(2)}) collective-permute-start(bf16[9,128,128]{2,1,0:T(8,128)(2,1)S(1)} %get-tuple-element.22), channel_id=1, source_target_pairs={{0,64},{32,96},{64,0},{96,32},{1,65},{33,97},{65,1},{97,33},{2,66}... | collective-permute-start | bytes 884744 | tf_op jit(solution)/shard_map/ppermute | solution.py:238
  40.7 13.3 %collective-permute-start.7 = (bf16[9,128,128]{2,1,0:T(8,128)(2,1)S(1)}, bf16[9,128,128]{2,1,0:T(8,128)(2,1)S(1)}, u32[]{:S(2)}, u32[]{:S(2)}) collective-permute-start(bf16[9,128,128]{2,1,0:T(8,128)(2,1)S(1)} %get-tuple-element.23), channel_id=1, source_target_pairs={{0,96},{32,0},{64,32},{96,64},{1,97},{33,1},{65,33},{97,65},{2,98}... | collective-permute-start | bytes 884744 | tf_op jit(solution)/shard_map/ppermute | solution.py:238
  42.1 4.8 %collective-permute-start.3 = (f32[8,128]{1,0:T(8,128)S(1)}, f32[8,128]{1,0:T(8,128)S(1)}, u32[]{:S(2)}, u32[]{:S(2)}) collective-permute-start(f32[8,128]{1,0:T(8,128)S(1)} %add.32), channel_id=1, source_target_pairs={{0,2},{2,4},{4,6},{6,0},{1,3},{3,5},{5,7},{7,1},{8,10},{10,12},{12... | collective-permute-start | bytes 12296 | tf_op jit(solution)/shard_map/ppermute | solution.py:238
  47.0 5.1 %collective-permute-start.4 = (f32[8,128]{1,0:T(8,128)S(1)}, f32[8,128]{1,0:T(8,128)S(1)}, u32[]{:S(2)}, u32[]{:S(2)}) collective-permute-start(f32[8,128]{1,0:T(8,128)S(1)} %add.33), channel_id=1, source_target_pairs={{0,4},{2,6},{4,0},{6,2},{1,5},{3,7},{5,1},{7,3},{8,12},{10,14},{12... | collective-permute-start | bytes 12296 | tf_op jit(solution)/shard_map/ppermute | solution.py:238
  54.2 15.4 %collective-permute-start.12 = (bf16[9,128,128]{2,1,0:T(8,128)(2,1)S(1)}, bf16[9,128,128]{2,1,0:T(8,128)(2,1)S(1)}, u32[]{:S(2)}, u32[]{:S(2)}) collective-permute-start(bf16[9,128,128]{2,1,0:T(8,128)(2,1)S(1)} %add_convert_fusion.own_ref), channel_id=1, source_target_pairs={{0,96},{32,0},{64,32},{96,64},{1,97},{33,1},{65,33},{97,65},{2,98}... | collective-permute-start | bytes 884744 | tf_op jit(solution)/shard_map/ppermute | solution.py:238
  56.5 13.1 %collective-permute-start.11 = (bf16[9,128,128]{2,1,0:T(8,128)(2,1)S(1)}, bf16[9,128,128]{2,1,0:T(8,128)(2,1)S(1)}, u32[]{:S(2)}, u32[]{:S(2)}) collective-permute-start(bf16[9,128,128]{2,1,0:T(8,128)(2,1)S(1)} %add_convert_fusion.own_ref), channel_id=1, source_target_pairs={{0,64},{32,96},{64,0},{96,32},{1,65},{33,97},{65,1},{97,33},{2,66}... | collective-permute-start | bytes 884744 | tf_op jit(solution)/shard_map/ppermute | solution.py:238
  57.7 15.2 %collective-permute-start.10 = (bf16[9,128,128]{2,1,0:T(8,128)(2,1)S(1)}, bf16[9,128,128]{2,1,0:T(8,128)(2,1)S(1)}, u32[]{:S(2)}, u32[]{:S(2)}) collective-permute-start(bf16[9,128,128]{2,1,0:T(8,128)(2,1)S(1)} %add_convert_fusion.own_ref), channel_id=1, source_target_pairs={{0,32},{32,64},{64,96},{96,0},{1,33},{33,65},{65,97},{97,1},{2,34}... | collective-permute-start | bytes 884744 | tf_op jit(solution)/shard_map/ppermute | solution.py:238
  58.3 4.8 %collective-permute-start.8 = (f32[8,128]{1,0:T(8,128)S(1)}, f32[8,128]{1,0:T(8,128)S(1)}, u32[]{:S(2)}, u32[]{:S(2)}) collective-permute-start(f32[8,128]{1,0:T(8,128)S(1)} %add.34), channel_id=1, source_target_pairs={{0,8},{8,16},{16,24},{24,0},{1,9},{9,17},{17,25},{25,1},{2,10},{10... | collective-permute-start | bytes 12296 | tf_op jit(solution)/shard_map/ppermute | solution.py:238
  63.2 5.1 %collective-permute-start.9 = (f32[8,128]{1,0:T(8,128)S(1)}, f32[8,128]{1,0:T(8,128)S(1)}, u32[]{:S(2)}, u32[]{:S(2)}) collective-permute-start(f32[8,128]{1,0:T(8,128)S(1)} %add.35), channel_id=1, source_target_pairs={{0,16},{8,24},{16,0},{24,8},{1,17},{9,25},{17,1},{25,9},{2,18},{10... | collective-permute-start | bytes 12296 | tf_op jit(solution)/shard_map/ppermute | solution.py:238

commit v2 on v1

v2 whole, which is shorter than its diff:
```python
import functools

import jax
import jax.numpy as jnp
from jax import lax
from jax.experimental import pallas as pl
from jax.experimental.pallas import tpu as pltpu
from jax.sharding import Mesh
from jax.sharding import PartitionSpec as P

SEQ = 64
ITERS = 4
ALL = ("side", "pair", "blk_0", "blk_1", "core")
OWNERS = ("pair", "blk_0", "blk_1")
TILE = 128
PIECES = 8

damping_rate = 0.5
power_steps = 3
STEP = 256


def mxu(a, b, dims):
    return lax.dot_general(a, b, (dims, ((), ())), preferred_element_type=jnp.float32)


def as_three(row):
    high = row.astype(jnp.bfloat16).astype(jnp.float32)
    rest = row - high
    mid = rest.astype(jnp.bfloat16).astype(jnp.float32)
    low = rest - mid
    turn = lax.broadcasted_iota(jnp.int32, (16, row.shape[1]), 0)
    rows = jnp.where(turn == 0, high, jnp.where(turn == 1, mid, jnp.where(turn == 2, low, 0.0)))
    return rows.astype(jnp.bfloat16)


def feature_kernel(
    act_ref, grad_ref, pa_ref, po_ref, out_ref, act_low, grad_low, feats, by_coord
):
    step = pl.program_id(0)
    steps = pl.num_programs(0)
    tokens = act_ref.shape[0]
    rows = pl.ds(pl.multiple_of(step * tokens, tokens), tokens)
    act_low[rows, :] = mxu(act_ref[...], pa_ref[...], ((1,), (0,))).astype(jnp.bfloat16)
    grad_low[rows, :] = mxu(grad_ref[...], po_ref[...], ((1,), (0,))).astype(jnp.bfloat16)
    blocks, examples, width = by_coord.shape
    per = width // grad_low.shape[1]
    cols = grad_low.shape[1]

    def eight(half):
        for e in range(8):
            at = pl.ds((half * 8 + e) * SEQ, SEQ)
            feats[e] = mxu(act_low[at, :], grad_low[at, :], ((0,), (0,)))
        turned = jnp.swapaxes(feats[...], 0, 1)
        turned = turned.reshape(blocks, per, 8, cols)
        for j in range(per):
            by_coord[:, half * 8 : half * 8 + 8, j * cols : (j + 1) * cols] = turned[:, j]

    @pl.when(step == steps // 2)
    def _():
        eight(0)

    @pl.when(step == steps - 1)
    def _():
        eight(1)
        acc = jnp.zeros((examples, width), jnp.float32)
        for k in range(blocks):
            low = by_coord[k].astype(jnp.bfloat16)
            out_ref[k, :, :width] = low
            wide = low.astype(jnp.float32)
            acc = acc + wide * wide
        part = jnp.zeros((8, TILE), jnp.float32)
        for r in range(0, examples, 8):
            for c in range(0, width, TILE):
                part = part + acc[r : r + 8, c : c + TILE]
        tail = as_three(jnp.sum(part, axis=0, keepdims=True))
        for k in range(blocks):
            out_ref[k, :, width:] = tail


def features_of(activations, out_grads, proj_act, proj_out, blocks):
    arguments = (activations, out_grads, proj_act, proj_out)
    tokens, depth = activations.shape
    examples = tokens // SEQ
    ra, rb = proj_act.shape[1], proj_out.shape[1]
    width = ra * rb // blocks
    steps = 4
    size = tokens // steps
    return pl.pallas_call(
        feature_kernel,
        grid=(steps,),
        in_specs=[
            pl.BlockSpec((size, depth), lambda i: (i, 0)),
            pl.BlockSpec((size, depth), lambda i: (i, 0)),
            pl.BlockSpec((depth, ra), lambda i: (0, 0), pipeline_mode=pl.Buffered(1)),
            pl.BlockSpec((depth, rb), lambda i: (0, 0), pipeline_mode=pl.Buffered(1)),
        ],
        out_specs=pl.BlockSpec((blocks, examples, width + TILE), lambda i: (0, 0, 0)),
        out_shape=jax.ShapeDtypeStruct((blocks, examples, width + TILE), jnp.bfloat16),
        scratch_shapes=[
            pltpu.VMEM((tokens, ra), jnp.bfloat16),
            pltpu.VMEM((tokens, rb), jnp.bfloat16),
            pltpu.VMEM((8, ra, rb), jnp.float32),
            pltpu.VMEM((blocks, examples, width), jnp.float32),
        ],
        compiler_params=pltpu.CompilerParams(
            dimension_semantics=("arbitrary",), vmem_limit_bytes=32 << 20
        ),
        name="features",
    )(*(pltpu.with_memory_space_constraint(x, pltpu.HBM) for x in arguments))


NEAR = ((0, 1), (0, 2), (0, 3), (1, 2), (1, 3))


def row_and_column(size=TILE):
    shape = (size, size)
    return lax.broadcasted_iota(jnp.int32, shape, 0), lax.broadcasted_iota(jnp.int32, shape, 1)


def tile_at(index, count=1):
    if isinstance(index, int):
        return slice(index * TILE, (index + count) * TILE)
    return pl.ds(pl.multiple_of(index * TILE, TILE), count * TILE)


def gram_kernel(core_ref, mine_ref, other_ref, own_ref, sum_ref, send_ref):
    core = core_ref[0]
    width = mine_ref.shape[1] - TILE
    squares = jnp.sum(
        mine_ref[:, width:].astype(jnp.float32) + other_ref[:, width:].astype(jnp.float32),
        axis=0,
        keepdims=True,
    )
    sum_ref[...] = jnp.broadcast_to(squares, sum_ref.shape)
    row, column = row_and_column()

    def product(left, right):
        dims = ((0,), (0,))
        return mxu(mine_ref[:, left], mine_ref[:, right], dims) + mxu(
            other_ref[:, left], other_ref[:, right], dims
        )

    diagonals = []
    for n in range(2):
        first = 4 * core + 2 * n
        left = tile_at(first, 2)
        near = product(left, left)
        after = product(left, tile_at(lax.rem(first + 2, 8), 2))
        far = product(tile_at(2 * n + core), tile_at(2 * n + 4, 2))
        packed = jnp.where(row <= column, near[:TILE, :TILE], near[TILE:, TILE:])
        inner = jnp.where(row == column, near[TILE:, TILE:], 0.0)
        diagonals.append(jnp.sum(inner, axis=0, keepdims=True))
        pieces = (
            packed,
            near[:TILE, TILE:],
            after[:TILE, :TILE],
            after[:TILE, TILE:],
            after[TILE:, :TILE],
            after[TILE:, TILE:],
            far[:, :TILE],
            far[:, TILE:],
        )
        for m, piece in enumerate(pieces):
            own_ref[tile_at(n * PIECES + m), :] = piece
            send_ref[tile_at(n * PIECES + m), :] = piece.astype(jnp.bfloat16)
    turn = lax.broadcasted_iota(jnp.int32, (16, TILE), 0)
    last = jnp.where(turn == 3, diagonals[0], jnp.where(turn == 4, diagonals[1], 0.0))
    rows = slice(2 * PIECES * TILE, 2 * PIECES * TILE + 16)
    own_ref[rows, :] = last
    send_ref[rows, :] = as_three(squares) + last.astype(jnp.bfloat16)


def gram_parts(core, mine, other):
    count = 2 * PIECES * TILE + 16
    vmem = pl.BlockSpec(memory_space=pltpu.VMEM)
    return pl.pallas_call(
        gram_kernel,
        in_specs=[pl.BlockSpec(memory_space=pltpu.SMEM), vmem, vmem],
        out_specs=[vmem, vmem, vmem],
        out_shape=[
            jax.ShapeDtypeStruct((count, TILE), jnp.float32),
            jax.ShapeDtypeStruct((8, TILE), jnp.float32),
            jax.ShapeDtypeStruct((count, TILE), jnp.bfloat16),
        ],
        compiler_params=pltpu.CompilerParams(vmem_limit_bytes=16 << 20),
        name="gram_parts",
    )(core, mine, other)


def put_pieces(half, ref, gram):
    row, column = row_and_column()
    last = ref[2 * PIECES * TILE :, :].astype(jnp.float32)
    for n in range(2):
        first = 4 * half + 2 * n
        packed = ref[tile_at(n * PIECES), :].astype(jnp.float32)
        turned = packed.T
        upper = jnp.where(row <= column, packed, turned)
        inner = jnp.where(row < column, turned, last[3 + n : 4 + n, :])
        lower = jnp.where(row > column, packed, inner)
        gram[tile_at(first), tile_at(first)] = upper.astype(jnp.bfloat16)
        gram[tile_at(first + 1), tile_at(first + 1)] = lower.astype(jnp.bfloat16)
        spots = [(lax.rem(first + i, 8), lax.rem(first + j, 8)) for i, j in NEAR]
        spots += [(2 * n + half, 2 * n + 4), (2 * n + half, 2 * n + 5)]
        for m, (i, j) in enumerate(spots):
            piece = ref[tile_at(n * PIECES + 1 + m), :]
            gram[tile_at(i), tile_at(j)] = piece
            gram[tile_at(j), tile_at(i)] = piece.T


def spread_kernel(core_ref, half_ref, gram_ref):
    put_pieces(core_ref[0], half_ref, gram_ref)


def spread(core, half, width):
    return pl.pallas_call(
        spread_kernel,
        in_specs=[pl.BlockSpec(memory_space=pltpu.SMEM), pl.BlockSpec(memory_space=pltpu.VMEM)],
        out_specs=pl.BlockSpec(memory_space=pltpu.VMEM),
        out_shape=jax.ShapeDtypeStruct((width, width), jnp.bfloat16),
        compiler_params=pltpu.CompilerParams(vmem_limit_bytes=16 << 20),
        name="spread",
    )(core, half)


def order_kernel(core_ref, mine_ref, other_ref, out_ref, ordered):
    core = core_ref[0]
    groups, width, examples = out_ref.shape
    piece = 16
    count = examples // (2 * piece)
    for g in range(groups):
        for p in range(count):
            at = slice((g * count + p) * piece, (g * count + p + 1) * piece)
            for which, ref in ((core, mine_ref), (1 - core, other_ref)):
                to = pl.multiple_of(p * 2 * piece + which * piece, piece)
                ordered[g, pl.ds(to, piece), :] = ref[at, :width]
        out_ref[g] = ordered[g].T


def in_order(core, mine, other, width):
    vmem = pl.BlockSpec(memory_space=pltpu.VMEM)
    examples = mine.shape[0]
    return pl.pallas_call(
        order_kernel,
        in_specs=[pl.BlockSpec(memory_space=pltpu.SMEM), vmem, vmem],
        out_specs=vmem,
        out_shape=jax.ShapeDtypeStruct((2, width, examples), jnp.bfloat16),
        scratch_shapes=[pltpu.VMEM((2, examples, width), jnp.bfloat16)],
        compiler_params=pltpu.CompilerParams(vmem_limit_bytes=16 << 20),
        name="in_order",
    )(core, mine, other)


def solve_kernel(
    coords,
    core_ref,
    sum_ref,
    far_sum_ref,
    rest_ref,
    started_ref,
    mine_ref,
    group_ref,
    out_ref,
    gram,
    first,
    second,
    low,
):
    put_pieces(1 - core_ref[0], rest_ref, gram)
    width = gram.shape[0]
    examples = mine_ref.shape[0]
    columns = [slice(c, c + STEP) for c in range(0, width, STEP)]

    def operate(field):
        for at in columns:
            yield at, mxu(field(), gram[:, at], ((1,), (0,)))

    vector = jnp.full((1, width), 1.0 / width**0.5, jnp.float32)
    for _ in range(power_steps):
        image = mxu(as_three(vector), gram[...], ((1,), (0,)))
        image = jnp.sum(image, axis=0, keepdims=True)
        radius = jnp.sqrt(jnp.sum(image * image, axis=1, keepdims=True) + 1e-06)
        vector = image / radius
    total = jnp.sum(sum_ref[0:1, :], axis=1, keepdims=True) + jnp.sum(
        jnp.sum(far_sum_ref[...].astype(jnp.float32)[0:3, :], axis=0, keepdims=True), axis=1, keepdims=True
    )
    damping = damping_rate * (total / coords)
    center = damping + radius
    strides = [1.0 / center]
    momenta = []
    for sweep in range(1, ITERS):
        if sweep == 1:
            momenta.append(0.5 * (radius * strides[-1]) ** 2)
        else:
            momenta.append((0.5 * radius * strides[-1]) ** 2)
        strides.append(1.0 / (center - momenta[-1] / strides[-1]))
    keep = [1.0 + m - s * damping for m, s in zip(momenta, strides)]
    weights = (
        strides[1] - strides[3] * momenta[1],
        strides[2] + strides[3] * keep[2],
        strides[3] * strides[2],
    )

    def right_side(at):
        return mine_ref[:, at].astype(jnp.float32)

    for at, value in operate(lambda: mine_ref[:, :width]):
        value = keep[0] * right_side(at) - strides[0] * value
        first[:, at] = value
        low[0, :, at] = value.astype(jnp.bfloat16)
    for at, value in operate(lambda: low[0]):
        value = keep[1] * first[:, at] - momenta[0] * right_side(at) - strides[1] * value
        second[:, at] = value
        low[1, :, at] = value.astype(jnp.bfloat16)
    for at, value in operate(lambda: low[1]):
        value = (
            strides[0] * right_side(at)
            + weights[0] * first[:, at]
            + weights[1] * second[:, at]
            - weights[2] * value
        )
        low[0, :, at] = value.astype(jnp.bfloat16)
    half = examples // 2
    for g in range(2):
        out_ref[g * half : (g + 1) * half, :] = mxu(
            low[0, g * half : (g + 1) * half, :],
            group_ref[g],
            ((1,), (0,)),
        ).astype(out_ref.dtype)


def block_scores(coords, core, squares, far_squares, rest, started, mine, rows):
    vmem = pl.BlockSpec(memory_space=pltpu.VMEM)
    smem = pl.BlockSpec(memory_space=pltpu.SMEM)
    examples = mine.shape[0]
    width = started.shape[0]
    field = (examples, width)
    return pl.pallas_call(
        functools.partial(solve_kernel, coords),
        in_specs=[smem] + [vmem] * 6,
        out_specs=[vmem, vmem],
        out_shape=[
            jax.ShapeDtypeStruct((examples, examples), jnp.bfloat16),
            jax.ShapeDtypeStruct((width, width), jnp.bfloat16),
        ],
        scratch_shapes=[
            pltpu.VMEM(field, jnp.float32),
            pltpu.VMEM(field, jnp.float32),
            pltpu.VMEM((2,) + field, jnp.bfloat16),
        ],
        input_output_aliases={4: 1},
        compiler_params=pltpu.CompilerParams(vmem_limit_bytes=32 << 20),
        name="solve",
    )(core, squares, far_squares, rest, started, mine, rows)[0]


def shifted(value, axis, shift):
    size = lax.axis_size(axis)
    return lax.ppermute(value, axis, [(i, (i + shift) % size) for i in range(size)])


def shards(activations, out_grads, proj_act, proj_out):
    examples = activations.shape[0] // SEQ
    coords = proj_act.shape[1] * proj_out.shape[1]
    blocks = lax.axis_size(OWNERS)
    by_block = features_of(activations, out_grads, proj_act, proj_out, blocks)
    arrived = lax.all_to_all(by_block, OWNERS, 0, 0, tiled=True)
    mine = arrived.reshape(blocks * examples, -1)
    other = shifted(mine, "core", 1)

    core = lax.axis_index("core").astype(jnp.int32).reshape(1)
    own, squares, send = gram_parts(core, mine, other)
    across = shifted(send, "side", 1)
    count = own.shape[0]
    width = coords // blocks
    mine_later, other_later, _ = lax.optimization_barrier((mine, other, send))
    rows = in_order(core, mine_later, other_later, width)
    half = (own + across.astype(jnp.float32)).astype(jnp.bfloat16)
    rest = shifted(half, "core", 1)
    started = spread(core, half, width)
    term = block_scores(coords, core, squares, across[count - 16 :], rest, started, mine, rows)
    terms = lax.all_to_all(term.reshape(blocks, examples, -1), OWNERS, 0, 0, tiled=True)
    scores = jnp.sum(terms.astype(jnp.float32), axis=0)
    return scores * float(examples * lax.axis_size(("side", "pair")))


def solution(mesh):
    split = Mesh(mesh.devices.reshape(2, 2, 4, 4, 2), ALL)
    placed = (P(ALL, None), P(ALL, None), P(), P())
    return jax.shard_map(shards, mesh=split, in_specs=placed, out_specs=P(ALL, None), check_vma=False)
```

time: 96.9 us -> 80.3 us (0.83); the launches traced: 95.7 us -> 80.2 us
  blocking collectives: 15.6 us -> 43.7 us
  waiting for transfers between devices: 38.2 us -> 16.5 us
  starting transfers between devices: 22.4 us -> 2.9 us
  Pallas kernels: 17.2 us -> 16.2 us
    all_to_all x1 -> x2, blocking collectives: 15.6 us -> 43.7 us  [the longest x1 28.2 us: shards(): arrived = lax.all_to_all(by_block, OWNERS, 0, 0, tiled=True)]
    ppermute x13 -> x3, waiting for transfers between devices: 32.1 us -> 16.5 us  [shifted(): lax.ppermute(value, axis, [(i, (i + shift) % size) for i in range(size)])]
    ppermute x13 -> x3, starting transfers between devices: 14 us -> 2.9 us  [shifted(): lax.ppermute(value, axis, [(i, (i + shift) % size) for i in range(size)])]
    all_to_all x1 -> x0, starting transfers between devices: 8.42 us -> none  [shards(): arrived = lax.all_to_all(by_block, BLK, 0, 0, tiled=True)]
    all_to_all x1 -> x0, waiting for transfers between devices: 6.16 us -> none  [shards(): arrived = lax.all_to_all(by_block, BLK, 0, 0, tiled=True)]
    pallas_call x1 -> x3, Pallas kernels: 6.57 us -> 6.78 us  [the longest x1 5.72 us: block_scores(): pl.pallas_call(functools.partial(solve_kernel, coords), in_specs=[smem] +...]
  transfers between devices with their start and end apart: 14 -> 3, of which waited for: 10 -> 3; matrix products, arithmetic and copies ran while one was open for 1% -> 0% of each run, Pallas kernels for 0% -> 1%
where the time goes in v2:
time: 80.3 us; the launch traced here: 80.2 us
  blocking collectives  43.7 us (54%)
  waiting for transfers between devices  16.5 us (21%)
  Pallas kernels  16.2 us (20%)
  starting transfers between devices  2.9 us (4%)
  other arithmetic  0.82 us (1%)
    all_to_all x1, blocking collectives, shards(): arrived = lax.all_to_all(by_block, OWNERS, 0, 0, tiled=True)  28.2 us
    ppermute x3, waiting for transfers between devices, shifted(): lax.ppermute(value, axis, [(i, (i + shift) % size) for i in range(size)])  16.5 us
    all_to_all x1, blocking collectives, shards(): lax.all_to_all(term.reshape(blocks, examples, -1), OWNERS, 0, 0, tiled=True)  15.4 us
    pallas_call x1, Pallas kernels, features_of(): pl.pallas_call(feature_kernel, grid=(steps,), in_specs=[pl.BlockSpec((siz...  8.54 us
    pallas_call x1, Pallas kernels, block_scores(): pl.pallas_call(functools.partial(solve_kernel, coords), in_specs=[smem] +...  5.72 us
    ppermute x3, starting transfers between devices, shifted(): lax.ppermute(value, axis, [(i, (i + shift) % size) for i in range(size)])  2.9 us
  transfers between devices with their start and end apart: 3, of which 3 were waited for; matrix products, arithmetic and copies ran while one was open for 0% of the time, Pallas kernels for 1%

profile of v2, /device:TPU:0, one launch (start us, length us, event | category | flops | bytes accessed | tf_op | source)
XLA Modules:
  0.0 80.2 jit_solution(15999490859769129541)
XLA Ops:
  0.0 8.5 %features.1 = bf16[32,16,1152]{2,1,0:T(8,128)(2,1)S(1)} custom-call(bf16[1024,3072]{1,0:T(8,128)(2,1)} %act_ref.1, bf16[1024,3072]{1,0:T(8,128)(2,1)} %grad_ref.1, bf16[3072,128]{1,0:T(8,128)(2,1)} %pa_ref.1, bf16[3072,256]{1,0:T(8,128)(2,1)} %po_ref.1), custom_call_target="tpu_custom_call" | custom-call | tf_op jit(solution)/shard_map/features/pallas_call | solution.py:89
  8.6 28.2 %all_to_all.10 = bf16[32,16,1152]{2,1,0:T(8,128)(2,1)S(1)} all-to-all(bf16[32,16,1152]{2,1,0:T(8,128)(2,1)S(1)} %features.1), channel_id=1, replica_groups=mesh['side'=2,'pair'=2,'blk_0'=4,'blk_1'=4,'core'=2] {'pair','blk_0','bl..., dimensions={0} | all-to-all | bytes 2359296 | tf_op jit(solution)/shard_map/all_to_all | solution.py:367
  36.8 0.0 collective-permute-start
  36.8 2.8 %collective-permute-done.other_ref = bf16[512,1152]{1,0:T(8,128)(2,1)S(1)} collective-permute-done((bf16[512,1152]{1,0:T(8,128)(2,1)S(1)}, bf16[512,1152]{1,0:T(8,128)(2,1)S(1)}, u32[]{:S(2)}, u32[]{:S(2)}) %collective-permute-start) | collective-permute-done | bytes 1179680 | tf_op jit(solution)/shard_map/ppermute | solution.py:359
  39.6 0.9 %gram_parts.1 = (f32[2064,128]{1,0:T(8,128)S(1)}, f32[8,128]{1,0:T(8,128)S(1)}, bf16[2064,128]{1,0:T(8,128)(2,1)S(1)}) custom-call(s32[1]{0:T(128)} %bitcast.core_ref, bf16[512,1152]{1,0:T(8,128)(2,1)S(1)} %bitcast.4, bf16[512,1152]{1,0:T(8,128)(2,1)S(1)} %collective-permute-done.other_ref), custom_call_target="tpu_custom_call" | custom-call | tf_op jit(solution)/shard_map/gram_parts/pallas_call | solution.py:177
  40.5 2.8 %collective-permute-start.1 = (bf16[2064,128]{1,0:T(8,128)(2,1)S(1)}, bf16[2064,128]{1,0:T(8,128)(2,1)S(1)}, u32[]{:S(2)}, u32[]{:S(2)}) collective-permute-start(bf16[2064,128]{1,0:T(8,128)(2,1)S(1)} %get-tuple-element.12), channel_id=1, source_target_pairs={{0,64},{64,0},{1,65},{65,1},{2,66},{66,2},{3,67},{67,3},{4,68},{68... | collective-permute-start | bytes 1585160 | tf_op jit(solution)/shard_map/ppermute | solution.py:359
  43.4 12.8 %collective-permute-done.1 = bf16[2064,128]{1,0:T(8,128)(2,1)S(1)} collective-permute-done((bf16[2064,128]{1,0:T(8,128)(2,1)S(1)}, bf16[2064,128]{1,0:T(8,128)(2,1)S(1)}, u32[]{:S(2)}, u32[]{:S(2)}) %collective-permute-start.1) | collective-permute-done | bytes 528416 | tf_op jit(solution)/shard_map/ppermute | solution.py:359
  56.2 0.1 add_convert_fusion.half_ref
  56.3 0.1 collective-permute-start.2
  56.4 0.7 in_order.1.group_ref
  57.1 0.4 spread.1.started_ref
  57.5 0.8 %collective-permute-done.2.rest_ref = bf16[2064,128]{1,0:T(8,128)(2,1)S(1)} collective-permute-done((bf16[2064,128]{1,0:T(8,128)(2,1)S(1)}, bf16[2064,128]{1,0:T(8,128)(2,1)S(1)}, u32[]{:S(2)}, u32[]{:S(2)}) %collective-permute-start.2) | collective-permute-done | bytes 528416 | tf_op jit(solution)/shard_map/ppermute | solution.py:359
  58.3 5.7 %solve.1 = (bf16[512,512]{1,0:T(8,128)(2,1)S(1)}, bf16[1024,1024]{1,0:T(8,128)(2,1)S(1)}) custom-call(s32[1]{0:T(128)} %bitcast.core_ref, f32[8,128]{1,0:T(8,128)S(1)} %get-tuple-element.11.sum_ref, bf16[16,128]{1,0:T(8,128)(2,1)S(1)} %slice.4.far_sum_ref, bf16[2064,128]{1,0:T(8,128)(2,1)S(1)} %collective-permute-done.2.rest_ref, ...), custom_call_target="tpu_custom_call", output_to_operand_aliasing={{1}: (4, {})} | custom-call | tf_op jit(solution)/shard_map/solve/pallas_call | solution.py:338
  64.0 15.4 %all_to_all.11 = bf16[32,16,512]{2,1,0:T(8,128)(2,1)S(1)} all-to-all(bf16[32,16,512]{2,1,0:T(8,128)(2,1)S(1)} %bitcast.7), channel_id=1, replica_groups=mesh['side'=2,'pair'=2,'blk_0'=4,'blk_1'=4,'core'=2] {'pair','blk_0','bl..., dimensions={0} | all-to-all | bytes 1048576 | tf_op jit(solution)/shard_map/all_to_all | solution.py:382
  79.4 0.1 convert_reduce_fusion
  79.5 0.6 broadcast_multiply_fusion
  (1 shorter events, 0.0 us)
Async XLA Ops:
  36.8 2.8 %collective-permute-start = (bf16[512,1152]{1,0:T(8,128)(2,1)S(1)}, bf16[512,1152]{1,0:T(8,128)(2,1)S(1)}, u32[]{:S(2)}, u32[]{:S(2)}) collective-permute-start(bf16[512,1152]{1,0:T(8,128)(2,1)S(1)} %bitcast.3), channel_id=1, source_target_pairs={{0,1},{1,0},{2,3},{3,2},{4,5},{5,4},{6,7},{7,6},{8,9},{9,8},{10,11... | collective-permute-start | bytes 3538952 | tf_op jit(solution)/shard_map/ppermute | solution.py:359
  40.5 15.6 %collective-permute-start.1 = (bf16[2064,128]{1,0:T(8,128)(2,1)S(1)}, bf16[2064,128]{1,0:T(8,128)(2,1)S(1)}, u32[]{:S(2)}, u32[]{:S(2)}) collective-permute-start(bf16[2064,128]{1,0:T(8,128)(2,1)S(1)} %get-tuple-element.12), channel_id=1, source_target_pairs={{0,64},{64,0},{1,65},{65,1},{2,66},{66,2},{3,67},{67,3},{4,68},{68... | collective-permute-start | bytes 1585160 | tf_op jit(solution)/shard_map/ppermute | solution.py:359
  56.3 2.0 %collective-permute-start.2 = (bf16[2064,128]{1,0:T(8,128)(2,1)S(1)}, bf16[2064,128]{1,0:T(8,128)(2,1)S(1)}, u32[]{:S(2)}, u32[]{:S(2)}) collective-permute-start(bf16[2064,128]{1,0:T(8,128)(2,1)S(1)} %add_convert_fusion.half_ref), channel_id=1, source_target_pairs={{0,1},{1,0},{2,3},{3,2},{4,5},{5,4},{6,7},{7,6},{8,9},{9,8},{10,11... | collective-permute-start | bytes 1585160 | tf_op jit(solution)/shard_map/ppermute | solution.py:359

commit v3 on v2

--- a/solution.py
+++ b/solution.py
@@ -35,7 +35,7 @@
 
 
 def feature_kernel(
-    act_ref, grad_ref, pa_ref, po_ref, out_ref, act_low, grad_low, feats, by_coord
+    side_ref, act_ref, grad_ref, pa_ref, po_ref, out_ref, act_low, grad_low, feats, by_coord
 ):
     step = pl.program_id(0)
     steps = pl.num_programs(0)
@@ -64,9 +64,10 @@
     def _():
         eight(1)
         acc = jnp.zeros((examples, width), jnp.float32)
+        turn = side_ref[0] * (blocks // 2)
         for k in range(blocks):
             low = by_coord[k].astype(jnp.bfloat16)
-            out_ref[k, :, :width] = low
+            out_ref[lax.rem(k + turn, blocks), :, :width] = low
             wide = low.astype(jnp.float32)
             acc = acc + wide * wide
         part = jnp.zeros((8, TILE), jnp.float32)
@@ -78,7 +79,7 @@
             out_ref[k, :, width:] = tail
 
 
-def features_of(activations, out_grads, proj_act, proj_out, blocks):
+def features_of(side, activations, out_grads, proj_act, proj_out, blocks):
     arguments = (activations, out_grads, proj_act, proj_out)
     tokens, depth = activations.shape
     examples = tokens // SEQ
@@ -90,6 +91,7 @@
         feature_kernel,
         grid=(steps,),
         in_specs=[
+            pl.BlockSpec(memory_space=pltpu.SMEM),
             pl.BlockSpec((size, depth), lambda i: (i, 0)),
             pl.BlockSpec((size, depth), lambda i: (i, 0)),
             pl.BlockSpec((depth, ra), lambda i: (0, 0), pipeline_mode=pl.Buffered(1)),
@@ -107,7 +109,7 @@
             dimension_semantics=("arbitrary",), vmem_limit_bytes=32 << 20
         ),
         name="features",
-    )(*(pltpu.with_memory_space_constraint(x, pltpu.HBM) for x in arguments))
+    )(side, *(pltpu.with_memory_space_constraint(x, pltpu.HBM) for x in arguments))
 
 
 NEAR = ((0, 1), (0, 2), (0, 3), (1, 2), (1, 3))
@@ -363,14 +365,15 @@
     examples = activations.shape[0] // SEQ
     coords = proj_act.shape[1] * proj_out.shape[1]
     blocks = lax.axis_size(OWNERS)
-    by_block = features_of(activations, out_grads, proj_act, proj_out, blocks)
+    side = lax.axis_index("side").astype(jnp.int32).reshape(1)
+    by_block = features_of(side, activations, out_grads, proj_act, proj_out, blocks)
     arrived = lax.all_to_all(by_block, OWNERS, 0, 0, tiled=True)
     mine = arrived.reshape(blocks * examples, -1)
     other = shifted(mine, "core", 1)
 
     core = lax.axis_index("core").astype(jnp.int32).reshape(1)
     own, squares, send = gram_parts(core, mine, other)
-    across = shifted(send, "side", 1)
+    across = lax.ppermute(send, ("side", "pair"), [(0, 3), (3, 0), (1, 2), (2, 1)])
     count = own.shape[0]
     width = coords // blocks
     mine_later, other_later, _ = lax.optimization_barrier((mine, other, send))

time: 80.3 us -> 80.1 us (level)
  starting transfers between devices: 2.9 us -> 2.06 us
    ppermute x0 -> x1, waiting for transfers between devices: none -> 13.4 us  [shards(): lax.ppermute(send, ('side', 'pair'), [(0, 3), (3, 0), (1, 2), (2, 1)])]
    ppermute x3 -> x2, waiting for transfers between devices: 16.5 us -> 3.67 us  [shifted(): lax.ppermute(value, axis, [(i, (i + shift) % size) for i in range(size)])]
    ppermute x3 -> x2, starting transfers between devices: 2.9 us -> 0.09 us  [shifted(): lax.ppermute(value, axis, [(i, (i + shift) % size) for i in range(size)])]
    ppermute x0 -> x1, starting transfers between devices: none -> 1.97 us  [shards(): lax.ppermute(send, ('side', 'pair'), [(0, 3), (3, 0), (1, 2), (2, 1)])]
where the time goes in v3:
time: 80.1 us; the launch traced here: 79.9 us
  blocking collectives  43.6 us (54%)
  waiting for transfers between devices  17 us (21%)
  Pallas kernels  16.3 us (20%)
  starting transfers between devices  2.06 us (3%)
  other arithmetic  0.82 us (1%)
    all_to_all x1, blocking collectives, shards(): arrived = lax.all_to_all(by_block, OWNERS, 0, 0, tiled=True)  28.2 us
    all_to_all x1, blocking collectives, shards(): lax.all_to_all(term.reshape(blocks, examples, -1), OWNERS, 0, 0, tiled=True)  15.4 us
    ppermute x1, waiting for transfers between devices, shards(): lax.ppermute(send, ('side', 'pair'), [(0, 3), (3, 0), (1, 2), (2, 1)])  13.4 us
    pallas_call x1, Pallas kernels, features_of(): pl.pallas_call(feature_kernel, grid=(steps,), in_specs=[pl.BlockSpec(memo...  8.6 us
    pallas_call x1, Pallas kernels, block_scores(): pl.pallas_call(functools.partial(solve_kernel, coords), in_specs=[smem] +...  5.72 us
    ppermute x2, waiting for transfers between devices, shifted(): lax.ppermute(value, axis, [(i, (i + shift) % size) for i in range(size)])  3.67 us
    ppermute x1, starting transfers between devices, shards(): lax.ppermute(send, ('side', 'pair'), [(0, 3), (3, 0), (1, 2), (2, 1)])  1.97 us
  transfers between devices with their start and end apart: 3, of which 3 were waited for; matrix products, arithmetic and copies ran while one was open for 0% of the time, Pallas kernels for 1%

profile of v3, /device:TPU:0, one launch (start us, length us, event | category | flops | bytes accessed | tf_op | source)
XLA Modules:
  0.0 79.9 jit_solution(11799228431684942270)
XLA Ops:
  0.0 8.6 %features.1 = bf16[32,16,1152]{2,1,0:T(8,128)(2,1)S(1)} custom-call(s32[1]{0:T(128)} %bitcast.1.side_ref, bf16[1024,3072]{1,0:T(8,128)(2,1)} %act_ref.1, bf16[1024,3072]{1,0:T(8,128)(2,1)} %grad_ref.1, bf16[3072,128]{1,0:T(8,128)(2,1)} %pa_ref.1, bf16[3072,256]{1,0:T(8,128)(2,1)} %po_ref.1), custom_call_target="tpu_custom_call" | custom-call | tf_op jit(solution)/shard_map/features/pallas_call | solution.py:90
  8.6 28.2 %all_to_all.10 = bf16[32,16,1152]{2,1,0:T(8,128)(2,1)S(1)} all-to-all(bf16[32,16,1152]{2,1,0:T(8,128)(2,1)S(1)} %features.1), channel_id=1, replica_groups=mesh['side'=2,'pair'=2,'blk_0'=4,'blk_1'=4,'core'=2] {'pair','blk_0','bl..., dimensions={0} | all-to-all | bytes 2359296 | tf_op jit(solution)/shard_map/all_to_all | solution.py:370
  36.8 0.0 collective-permute-start
  36.9 2.8 %collective-permute-done.other_ref = bf16[512,1152]{1,0:T(8,128)(2,1)S(1)} collective-permute-done((bf16[512,1152]{1,0:T(8,128)(2,1)S(1)}, bf16[512,1152]{1,0:T(8,128)(2,1)S(1)}, u32[]{:S(2)}, u32[]{:S(2)}) %collective-permute-start) | collective-permute-done | bytes 1179680 | tf_op jit(solution)/shard_map/ppermute | solution.py:361
  39.7 0.9 %gram_parts.1 = (f32[2064,128]{1,0:T(8,128)S(1)}, f32[8,128]{1,0:T(8,128)S(1)}, bf16[2064,128]{1,0:T(8,128)(2,1)S(1)}) custom-call(s32[1]{0:T(128)} %bitcast.core_ref, bf16[512,1152]{1,0:T(8,128)(2,1)S(1)} %bitcast.5, bf16[512,1152]{1,0:T(8,128)(2,1)S(1)} %collective-permute-done.other_ref), custom_call_target="tpu_custom_call" | custom-call | tf_op jit(solution)/shard_map/gram_parts/pallas_call | solution.py:179
  40.6 2.0 %collective-permute-start.1 = (bf16[2064,128]{1,0:T(8,128)(2,1)S(1)}, bf16[2064,128]{1,0:T(8,128)(2,1)S(1)}, u32[]{:S(2)}, u32[]{:S(2)}) collective-permute-start(bf16[2064,128]{1,0:T(8,128)(2,1)S(1)} %get-tuple-element.12), channel_id=1, source_target_pairs={{0,96},{96,0},{32,64},{64,32},{1,97},{97,1},{33,65},{65,33},{2,98}... | collective-permute-start | bytes 1585160 | tf_op jit(solution)/shard_map/ppermute | solution.py:376
  42.6 13.4 %collective-permute-done.1 = bf16[2064,128]{1,0:T(8,128)(2,1)S(1)} collective-permute-done((bf16[2064,128]{1,0:T(8,128)(2,1)S(1)}, bf16[2064,128]{1,0:T(8,128)(2,1)S(1)}, u32[]{:S(2)}, u32[]{:S(2)}) %collective-permute-start.1) | collective-permute-done | bytes 528416 | tf_op jit(solution)/shard_map/ppermute | solution.py:376
  55.9 0.1 add_convert_fusion.half_ref
  56.1 0.1 collective-permute-start.2
  56.2 0.7 in_order.1.group_ref
  56.9 0.4 spread.1.started_ref
  57.2 0.8 %collective-permute-done.2.rest_ref = bf16[2064,128]{1,0:T(8,128)(2,1)S(1)} collective-permute-done((bf16[2064,128]{1,0:T(8,128)(2,1)S(1)}, bf16[2064,128]{1,0:T(8,128)(2,1)S(1)}, u32[]{:S(2)}, u32[]{:S(2)}) %collective-permute-start.2) | collective-permute-done | bytes 528416 | tf_op jit(solution)/shard_map/ppermute | solution.py:361
  58.1 5.7 %solve.1 = (bf16[512,512]{1,0:T(8,128)(2,1)S(1)}, bf16[1024,1024]{1,0:T(8,128)(2,1)S(1)}) custom-call(s32[1]{0:T(128)} %bitcast.core_ref, f32[8,128]{1,0:T(8,128)S(1)} %get-tuple-element.11.sum_ref, bf16[16,128]{1,0:T(8,128)(2,1)S(1)} %slice.4.far_sum_ref, bf16[2064,128]{1,0:T(8,128)(2,1)S(1)} %collective-permute-done.2.rest_ref, ...), custom_call_target="tpu_custom_call", output_to_operand_aliasing={{1}: (4, {})} | custom-call | tf_op jit(solution)/shard_map/solve/pallas_call | solution.py:340
  63.8 15.4 %all_to_all.11 = bf16[32,16,512]{2,1,0:T(8,128)(2,1)S(1)} all-to-all(bf16[32,16,512]{2,1,0:T(8,128)(2,1)S(1)} %bitcast.8), channel_id=1, replica_groups=mesh['side'=2,'pair'=2,'blk_0'=4,'blk_1'=4,'core'=2] {'pair','blk_0','bl..., dimensions={0} | all-to-all | bytes 1048576 | tf_op jit(solution)/shard_map/all_to_all | solution.py:385
  79.2 0.1 convert_reduce_fusion
  79.3 0.6 broadcast_multiply_fusion
  (1 shorter events, 0.0 us)
Async XLA Ops:
  36.8 2.8 %collective-permute-start = (bf16[512,1152]{1,0:T(8,128)(2,1)S(1)}, bf16[512,1152]{1,0:T(8,128)(2,1)S(1)}, u32[]{:S(2)}, u32[]{:S(2)}) collective-permute-start(bf16[512,1152]{1,0:T(8,128)(2,1)S(1)} %bitcast.4), channel_id=1, source_target_pairs={{0,1},{1,0},{2,3},{3,2},{4,5},{5,4},{6,7},{7,6},{8,9},{9,8},{10,11... | collective-permute-start | bytes 3538952 | tf_op jit(solution)/shard_map/ppermute | solution.py:361
  40.6 15.3 %collective-permute-start.1 = (bf16[2064,128]{1,0:T(8,128)(2,1)S(1)}, bf16[2064,128]{1,0:T(8,128)(2,1)S(1)}, u32[]{:S(2)}, u32[]{:S(2)}) collective-permute-start(bf16[2064,128]{1,0:T(8,128)(2,1)S(1)} %get-tuple-element.12), channel_id=1, source_target_pairs={{0,96},{96,0},{32,64},{64,32},{1,97},{97,1},{33,65},{65,33},{2,98}... | collective-permute-start | bytes 1585160 | tf_op jit(solution)/shard_map/ppermute | solution.py:376
  56.1 2.0 %collective-permute-start.2 = (bf16[2064,128]{1,0:T(8,128)(2,1)S(1)}, bf16[2064,128]{1,0:T(8,128)(2,1)S(1)}, u32[]{:S(2)}, u32[]{:S(2)}) collective-permute-start(bf16[2064,128]{1,0:T(8,128)(2,1)S(1)} %add_convert_fusion.half_ref), channel_id=1, source_target_pairs={{0,1},{1,0},{2,3},{3,2},{4,5},{5,4},{6,7},{7,6},{8,9},{9,8},{10,11... | collective-permute-start | bytes 1585160 | tf_op jit(solution)/shard_map/ppermute | solution.py:361

commit v4 on v3

--- a/solution.py
+++ b/solution.py
@@ -85,7 +85,7 @@
     examples = tokens // SEQ
     ra, rb = proj_act.shape[1], proj_out.shape[1]
     width = ra * rb // blocks
-    steps = 4
+    steps = 2
     size = tokens // steps
     return pl.pallas_call(
         feature_kernel,
@@ -126,30 +126,43 @@
     return pl.ds(pl.multiple_of(index * TILE, TILE), count * TILE)
 
 
-def gram_kernel(core_ref, mine_ref, other_ref, own_ref, sum_ref, send_ref):
-    core = core_ref[0]
-    width = mine_ref.shape[1] - TILE
+def gram_products(core, rows_ref):
+    def product(left, right):
+        return mxu(rows_ref[:, left], rows_ref[:, right], ((0,), (0,)))
+
+    for n in range(2):
+        first = 4 * core + 2 * n
+        left = tile_at(first, 2)
+        yield n, 0, product(left, left)
+        yield n, 1, product(left, tile_at(lax.rem(first + 2, 8), 2))
+        yield n, 2, product(tile_at(2 * n + core), tile_at(2 * n + 4, 2))
+
+
+def part_of(n, m):
+    first = (5 * n + 2 * m) * TILE
+    return slice(first, first + (TILE if m == 2 else 2 * TILE))
+
+
+def own_gram_kernel(core_ref, mine_ref, acc_ref):
+    for n, m, value in gram_products(core_ref[0], mine_ref):
+        acc_ref[part_of(n, m), :] = value
+
+
+def gram_kernel(core_ref, acc_ref, mine_sum_ref, other_ref, own_ref, sum_ref, send_ref):
+    width = other_ref.shape[1] - TILE
     squares = jnp.sum(
-        mine_ref[:, width:].astype(jnp.float32) + other_ref[:, width:].astype(jnp.float32),
+        mine_sum_ref[...].astype(jnp.float32) + other_ref[:, width:].astype(jnp.float32),
         axis=0,
         keepdims=True,
     )
     sum_ref[...] = jnp.broadcast_to(squares, sum_ref.shape)
     row, column = row_and_column()
-
-    def product(left, right):
-        dims = ((0,), (0,))
-        return mxu(mine_ref[:, left], mine_ref[:, right], dims) + mxu(
-            other_ref[:, left], other_ref[:, right], dims
-        )
-
+    parts = {}
+    for n, m, value in gram_products(core_ref[0], other_ref):
+        parts[n, m] = acc_ref[part_of(n, m), :] + value
     diagonals = []
     for n in range(2):
-        first = 4 * core + 2 * n
-        left = tile_at(first, 2)
-        near = product(left, left)
-        after = product(left, tile_at(lax.rem(first + 2, 8), 2))
-        far = product(tile_at(2 * n + core), tile_at(2 * n + 4, 2))
+        near, after, far = parts[n, 0], parts[n, 1], parts[n, 2]
         packed = jnp.where(row <= column, near[:TILE, :TILE], near[TILE:, TILE:])
         inner = jnp.where(row == column, near[TILE:, TILE:], 0.0)
         diagonals.append(jnp.sum(inner, axis=0, keepdims=True))
@@ -176,18 +189,28 @@
 def gram_parts(core, mine, other):
     count = 2 * PIECES * TILE + 16
     vmem = pl.BlockSpec(memory_space=pltpu.VMEM)
+    smem = pl.BlockSpec(memory_space=pltpu.SMEM)
+    params = pltpu.CompilerParams(vmem_limit_bytes=16 << 20)
+    acc = pl.pallas_call(
+        own_gram_kernel,
+        in_specs=[smem, vmem],
+        out_specs=vmem,
+        out_shape=jax.ShapeDtypeStruct((10 * TILE, 2 * TILE), jnp.float32),
+        compiler_params=params,
+        name="own_gram",
+    )(core, mine)
     return pl.pallas_call(
         gram_kernel,
-        in_specs=[pl.BlockSpec(memory_space=pltpu.SMEM), vmem, vmem],
+        in_specs=[smem, vmem, vmem, vmem],
         out_specs=[vmem, vmem, vmem],
         out_shape=[
             jax.ShapeDtypeStruct((count, TILE), jnp.float32),
             jax.ShapeDtypeStruct((8, TILE), jnp.float32),
             jax.ShapeDtypeStruct((count, TILE), jnp.bfloat16),
         ],
-        compiler_params=pltpu.CompilerParams(vmem_limit_bytes=16 << 20),
+        compiler_params=params,
         name="gram_parts",
-    )(core, mine, other)
+    )(core, acc, mine[:, mine.shape[1] - TILE :], other)
 
 
 def put_pieces(half, ref, gram):
@@ -284,7 +307,9 @@
         radius = jnp.sqrt(jnp.sum(image * image, axis=1, keepdims=True) + 1e-06)
         vector = image / radius
     total = jnp.sum(sum_ref[0:1, :], axis=1, keepdims=True) + jnp.sum(
-        jnp.sum(far_sum_ref[...].astype(jnp.float32)[0:3, :], axis=0, keepdims=True), axis=1, keepdims=True
+        jnp.sum(far_sum_ref[...].astype(jnp.float32)[0:3, :], axis=0, keepdims=True),
+        axis=1,
+        keepdims=True,
     )
     damping = damping_rate * (total / coords)
     center = damping + radius

time: 80.1 us -> 79.2 us (0.989)
  transfers between devices with their start and end apart: 3 -> 3, of which waited for: 3 -> 3; matrix products, arithmetic and copies ran while one was open for 0% -> 0% of each run, Pallas kernels for 1% -> 2%
where the time goes in v4:
time: 79.2 us; the launch traced here: 79 us
  blocking collectives  43.6 us (55%)
  waiting for transfers between devices  16.4 us (21%)
  Pallas kernels  15.9 us (20%)
  starting transfers between devices  2.07 us (3%)
  other arithmetic  0.81 us (1%)
    all_to_all x1, blocking collectives, shards(): arrived = lax.all_to_all(by_block, OWNERS, 0, 0, tiled=True)  28.2 us
    all_to_all x1, blocking collectives, shards(): lax.all_to_all(term.reshape(blocks, examples, -1), OWNERS, 0, 0, tiled=True)  15.4 us
    ppermute x1, waiting for transfers between devices, shards(): lax.ppermute(send, ('side', 'pair'), [(0, 3), (3, 0), (1, 2), (2, 1)])  13.4 us
    pallas_call x1, Pallas kernels, features_of(): pl.pallas_call(feature_kernel, grid=(steps,), in_specs=[pl.BlockSpec(memo...  8.04 us
    pallas_call x1, Pallas kernels, block_scores(): pl.pallas_call(functools.partial(solve_kernel, coords), in_specs=[smem] +...  5.72 us
    ppermute x2, waiting for transfers between devices, shifted(): lax.ppermute(value, axis, [(i, (i + shift) % size) for i in range(size)])  3.09 us
    ppermute x1, starting transfers between devices, shards(): lax.ppermute(send, ('side', 'pair'), [(0, 3), (3, 0), (1, 2), (2, 1)])  1.98 us
  transfers between devices with their start and end apart: 3, of which 3 were waited for; matrix products, arithmetic and copies ran while one was open for 0% of the time, Pallas kernels for 2%

profile of v4, /device:TPU:0, one launch (start us, length us, event | category | flops | bytes accessed | tf_op | source)
XLA Modules:
  0.0 79.0 jit_solution(17266361354781866535)
XLA Ops:
  0.0 8.0 %features.1 = bf16[32,16,1152]{2,1,0:T(8,128)(2,1)S(1)} custom-call(s32[1]{0:T(128)} %bitcast.1.side_ref, bf16[1024,3072]{1,0:T(8,128)(2,1)} %act_ref.1, bf16[1024,3072]{1,0:T(8,128)(2,1)} %grad_ref.1, bf16[3072,128]{1,0:T(8,128)(2,1)} %pa_ref.1, bf16[3072,256]{1,0:T(8,128)(2,1)} %po_ref.1), custom_call_target="tpu_custom_call" | custom-call | tf_op jit(solution)/shard_map/features/pallas_call | solution.py:90
  8.1 28.2 %all_to_all.10 = bf16[32,16,1152]{2,1,0:T(8,128)(2,1)S(1)} all-to-all(bf16[32,16,1152]{2,1,0:T(8,128)(2,1)S(1)} %features.1), channel_id=1, replica_groups=mesh['side'=2,'pair'=2,'blk_0'=4,'blk_1'=4,'core'=2] {'pair','blk_0','bl..., dimensions={0} | all-to-all | bytes 2359296 | tf_op jit(solution)/shard_map/all_to_all | solution.py:395
  36.3 0.0 collective-permute-start
  36.3 0.6 own_gram.1.acc_ref
  36.9 2.3 %collective-permute-done.other_ref = bf16[512,1152]{1,0:T(8,128)(2,1)S(1)} collective-permute-done((bf16[512,1152]{1,0:T(8,128)(2,1)S(1)}, bf16[512,1152]{1,0:T(8,128)(2,1)S(1)}, u32[]{:S(2)}, u32[]{:S(2)}) %collective-permute-start) | collective-permute-done | bytes 1179680 | tf_op jit(solution)/shard_map/ppermute | solution.py:386
  39.1 0.6 gram_parts.1
  39.7 2.0 %collective-permute-start.1 = (bf16[2064,128]{1,0:T(8,128)(2,1)S(1)}, bf16[2064,128]{1,0:T(8,128)(2,1)S(1)}, u32[]{:S(2)}, u32[]{:S(2)}) collective-permute-start(bf16[2064,128]{1,0:T(8,128)(2,1)S(1)} %get-tuple-element.12), channel_id=1, source_target_pairs={{0,96},{96,0},{32,64},{64,32},{1,97},{97,1},{33,65},{65,33},{2,98}... | collective-permute-start | bytes 1585160 | tf_op jit(solution)/shard_map/ppermute | solution.py:401
  41.7 13.4 %collective-permute-done.1 = bf16[2064,128]{1,0:T(8,128)(2,1)S(1)} collective-permute-done((bf16[2064,128]{1,0:T(8,128)(2,1)S(1)}, bf16[2064,128]{1,0:T(8,128)(2,1)S(1)}, u32[]{:S(2)}, u32[]{:S(2)}) %collective-permute-start.1) | collective-permute-done | bytes 528416 | tf_op jit(solution)/shard_map/ppermute | solution.py:401
  55.1 0.1 add_convert_fusion.half_ref
  55.2 0.1 collective-permute-start.2
  55.3 0.7 in_order.1.group_ref
  56.0 0.4 spread.1.started_ref
  56.3 0.8 %collective-permute-done.2.rest_ref = bf16[2064,128]{1,0:T(8,128)(2,1)S(1)} collective-permute-done((bf16[2064,128]{1,0:T(8,128)(2,1)S(1)}, bf16[2064,128]{1,0:T(8,128)(2,1)S(1)}, u32[]{:S(2)}, u32[]{:S(2)}) %collective-permute-start.2) | collective-permute-done | bytes 528416 | tf_op jit(solution)/shard_map/ppermute | solution.py:386
  57.2 5.7 %solve.1 = (bf16[512,512]{1,0:T(8,128)(2,1)S(1)}, bf16[1024,1024]{1,0:T(8,128)(2,1)S(1)}) custom-call(s32[1]{0:T(128)} %bitcast.core_ref, f32[8,128]{1,0:T(8,128)S(1)} %get-tuple-element.11.sum_ref, bf16[16,128]{1,0:T(8,128)(2,1)S(1)} %slice.9.far_sum_ref, bf16[2064,128]{1,0:T(8,128)(2,1)S(1)} %collective-permute-done.2.rest_ref, ...), custom_call_target="tpu_custom_call", output_to_operand_aliasing={{1}: (4, {})} | custom-call | tf_op jit(solution)/shard_map/solve/pallas_call | solution.py:365
  62.9 15.4 %all_to_all.11 = bf16[32,16,512]{2,1,0:T(8,128)(2,1)S(1)} all-to-all(bf16[32,16,512]{2,1,0:T(8,128)(2,1)S(1)} %bitcast.9), channel_id=1, replica_groups=mesh['side'=2,'pair'=2,'blk_0'=4,'blk_1'=4,'core'=2] {'pair','blk_0','bl..., dimensions={0} | all-to-all | bytes 1048576 | tf_op jit(solution)/shard_map/all_to_all | solution.py:410
  78.3 0.1 convert_reduce_fusion
  78.4 0.6 broadcast_multiply_fusion
  (2 shorter events, 0.0 us)
Async XLA Ops:
  36.3 2.8 %collective-permute-start = (bf16[512,1152]{1,0:T(8,128)(2,1)S(1)}, bf16[512,1152]{1,0:T(8,128)(2,1)S(1)}, u32[]{:S(2)}, u32[]{:S(2)}) collective-permute-start(bf16[512,1152]{1,0:T(8,128)(2,1)S(1)} %bitcast.4), channel_id=1, source_target_pairs={{0,1},{1,0},{2,3},{3,2},{4,5},{5,4},{6,7},{7,6},{8,9},{9,8},{10,11... | collective-permute-start | bytes 3538952 | tf_op jit(solution)/shard_map/ppermute | solution.py:386
  39.7 15.3 %collective-permute-start.1 = (bf16[2064,128]{1,0:T(8,128)(2,1)S(1)}, bf16[2064,128]{1,0:T(8,128)(2,1)S(1)}, u32[]{:S(2)}, u32[]{:S(2)}) collective-permute-start(bf16[2064,128]{1,0:T(8,128)(2,1)S(1)} %get-tuple-element.12), channel_id=1, source_target_pairs={{0,96},{96,0},{32,64},{64,32},{1,97},{97,1},{33,65},{65,33},{2,98}... | collective-permute-start | bytes 1585160 | tf_op jit(solution)/shard_map/ppermute | solution.py:401
  55.2 2.0 %collective-permute-start.2 = (bf16[2064,128]{1,0:T(8,128)(2,1)S(1)}, bf16[2064,128]{1,0:T(8,128)(2,1)S(1)}, u32[]{:S(2)}, u32[]{:S(2)}) collective-permute-start(bf16[2064,128]{1,0:T(8,128)(2,1)S(1)} %add_convert_fusion.half_ref), channel_id=1, source_target_pairs={{0,1},{1,0},{2,3},{3,2},{4,5},{5,4},{6,7},{7,6},{8,9},{9,8},{10,11... | collective-permute-start | bytes 1585160 | tf_op jit(solution)/shard_map/ppermute | solution.py:386

commit v5 on v4

--- a/solution.py
+++ b/solution.py
@@ -148,7 +148,9 @@
         acc_ref[part_of(n, m), :] = value
 
 
-def gram_kernel(core_ref, acc_ref, mine_sum_ref, other_ref, own_ref, sum_ref, send_ref):
+def gram_kernel(
+    core_ref, acc_ref, mine_sum_ref, other_ref, own_a_ref, own_b_ref, sum_ref, send_a_ref, send_b_ref
+):
     width = other_ref.shape[1] - TILE
     squares = jnp.sum(
         mine_sum_ref[...].astype(jnp.float32) + other_ref[:, width:].astype(jnp.float32),
@@ -160,12 +162,11 @@
     parts = {}
     for n, m, value in gram_products(core_ref[0], other_ref):
         parts[n, m] = acc_ref[part_of(n, m), :] + value
-    diagonals = []
-    for n in range(2):
+    for n, (own_ref, send_ref) in enumerate(((own_a_ref, send_a_ref), (own_b_ref, send_b_ref))):
         near, after, far = parts[n, 0], parts[n, 1], parts[n, 2]
         packed = jnp.where(row <= column, near[:TILE, :TILE], near[TILE:, TILE:])
         inner = jnp.where(row == column, near[TILE:, TILE:], 0.0)
-        diagonals.append(jnp.sum(inner, axis=0, keepdims=True))
+        diagonal = jnp.sum(inner, axis=0, keepdims=True)
         pieces = (
             packed,
             near[:TILE, TILE:],
@@ -177,17 +178,17 @@
             far[:, TILE:],
         )
         for m, piece in enumerate(pieces):
-            own_ref[tile_at(n * PIECES + m), :] = piece
-            send_ref[tile_at(n * PIECES + m), :] = piece.astype(jnp.bfloat16)
-    turn = lax.broadcasted_iota(jnp.int32, (16, TILE), 0)
-    last = jnp.where(turn == 3, diagonals[0], jnp.where(turn == 4, diagonals[1], 0.0))
-    rows = slice(2 * PIECES * TILE, 2 * PIECES * TILE + 16)
-    own_ref[rows, :] = last
-    send_ref[rows, :] = as_three(squares) + last.astype(jnp.bfloat16)
+            own_ref[tile_at(m), :] = piece
+            send_ref[tile_at(m), :] = piece.astype(jnp.bfloat16)
+        turn = lax.broadcasted_iota(jnp.int32, (16, TILE), 0)
+        last = jnp.where(turn == 3, diagonal, 0.0)
+        rows = slice(PIECES * TILE, PIECES * TILE + 16)
+        own_ref[rows, :] = last
+        send_ref[rows, :] = as_three(squares) + last.astype(jnp.bfloat16)
 
 
 def gram_parts(core, mine, other):
-    count = 2 * PIECES * TILE + 16
+    count = PIECES * TILE + 16
     vmem = pl.BlockSpec(memory_space=pltpu.VMEM)
     smem = pl.BlockSpec(memory_space=pltpu.SMEM)
     params = pltpu.CompilerParams(vmem_limit_bytes=16 << 20)
@@ -202,10 +203,12 @@
     return pl.pallas_call(
         gram_kernel,
         in_specs=[smem, vmem, vmem, vmem],
-        out_specs=[vmem, vmem, vmem],
+        out_specs=[vmem] * 5,
         out_shape=[
             jax.ShapeDtypeStruct((count, TILE), jnp.float32),
+            jax.ShapeDtypeStruct((count, TILE), jnp.float32),
             jax.ShapeDtypeStruct((8, TILE), jnp.float32),
+            jax.ShapeDtypeStruct((count, TILE), jnp.bfloat16),
             jax.ShapeDtypeStruct((count, TILE), jnp.bfloat16),
         ],
         compiler_params=params,
@@ -213,39 +216,57 @@
     )(core, acc, mine[:, mine.shape[1] - TILE :], other)
 
 
-def put_pieces(half, ref, gram):
+def put_pieces(half, n, ref, gram):
     row, column = row_and_column()
-    last = ref[2 * PIECES * TILE :, :].astype(jnp.float32)
-    for n in range(2):
-        first = 4 * half + 2 * n
-        packed = ref[tile_at(n * PIECES), :].astype(jnp.float32)
-        turned = packed.T
-        upper = jnp.where(row <= column, packed, turned)
-        inner = jnp.where(row < column, turned, last[3 + n : 4 + n, :])
-        lower = jnp.where(row > column, packed, inner)
-        gram[tile_at(first), tile_at(first)] = upper.astype(jnp.bfloat16)
-        gram[tile_at(first + 1), tile_at(first + 1)] = lower.astype(jnp.bfloat16)
-        spots = [(lax.rem(first + i, 8), lax.rem(first + j, 8)) for i, j in NEAR]
-        spots += [(2 * n + half, 2 * n + 4), (2 * n + half, 2 * n + 5)]
-        for m, (i, j) in enumerate(spots):
-            piece = ref[tile_at(n * PIECES + 1 + m), :]
-            gram[tile_at(i), tile_at(j)] = piece
-            gram[tile_at(j), tile_at(i)] = piece.T
-
-
-def spread_kernel(core_ref, half_ref, gram_ref):
-    put_pieces(core_ref[0], half_ref, gram_ref)
-
-
-def spread(core, half, width):
+    last = ref[PIECES * TILE :, :].astype(jnp.float32)
+    first = 4 * half + 2 * n
+    packed = ref[tile_at(0), :].astype(jnp.float32)
+    turned = packed.T
+    upper = jnp.where(row <= column, packed, turned)
+    inner = jnp.where(row < column, turned, last[3:4, :])
+    lower = jnp.where(row > column, packed, inner)
+    gram[tile_at(first), tile_at(first)] = upper.astype(jnp.bfloat16)
+    gram[tile_at(first + 1), tile_at(first + 1)] = lower.astype(jnp.bfloat16)
+    spots = [(lax.rem(first + i, 8), lax.rem(first + j, 8)) for i, j in NEAR]
+    spots += [(2 * n + half, 2 * n + 4), (2 * n + half, 2 * n + 5)]
+    for m, (i, j) in enumerate(spots):
+        piece = ref[tile_at(1 + m), :]
+        gram[tile_at(i), tile_at(j)] = piece
+        gram[tile_at(j), tile_at(i)] = piece.T
+
+
+def spread_kernel(core_ref, half_ref, rest_ref, gram_ref):
+    put_pieces(core_ref[0], 0, half_ref, gram_ref)
+    put_pieces(1 - core_ref[0], 0, rest_ref, gram_ref)
+
+
+def spread(core, half, rest, width):
+    vmem = pl.BlockSpec(memory_space=pltpu.VMEM)
     return pl.pallas_call(
         spread_kernel,
-        in_specs=[pl.BlockSpec(memory_space=pltpu.SMEM), pl.BlockSpec(memory_space=pltpu.VMEM)],
-        out_specs=pl.BlockSpec(memory_space=pltpu.VMEM),
+        in_specs=[pl.BlockSpec(memory_space=pltpu.SMEM), vmem, vmem],
+        out_specs=vmem,
         out_shape=jax.ShapeDtypeStruct((width, width), jnp.bfloat16),
         compiler_params=pltpu.CompilerParams(vmem_limit_bytes=16 << 20),
         name="spread",
-    )(core, half)
+    )(core, half, rest)
+
+
+def spread_on_kernel(core_ref, half_ref, started_ref, gram_ref):
+    put_pieces(core_ref[0], 1, half_ref, gram_ref)
+
+
+def spread_on(core, half, started):
+    vmem = pl.BlockSpec(memory_space=pltpu.VMEM)
+    return pl.pallas_call(
+        spread_on_kernel,
+        in_specs=[pl.BlockSpec(memory_space=pltpu.SMEM), vmem, vmem],
+        out_specs=vmem,
+        out_shape=jax.ShapeDtypeStruct(started.shape, jnp.bfloat16),
+        input_output_aliases={2: 0},
+        compiler_params=pltpu.CompilerParams(vmem_limit_bytes=16 << 20),
+        name="spread_on",
+    )(core, half, started)
 
 
 def order_kernel(core_ref, mine_ref, other_ref, out_ref, ordered):
@@ -291,7 +312,7 @@
     second,
     low,
 ):
-    put_pieces(1 - core_ref[0], rest_ref, gram)
+    put_pieces(1 - core_ref[0], 1, rest_ref, gram)
     width = gram.shape[0]
     examples = mine_ref.shape[0]
     columns = [slice(c, c + STEP) for c in range(0, width, STEP)]
@@ -386,6 +407,10 @@
     return lax.ppermute(value, axis, [(i, (i + shift) % size) for i in range(size)])
 
 
+def to_other_owner(value):
+    return lax.ppermute(value, ("side", "pair"), [(0, 3), (3, 0), (1, 2), (2, 1)])
+
+
 def shards(activations, out_grads, proj_act, proj_out):
     examples = activations.shape[0] // SEQ
     coords = proj_act.shape[1] * proj_out.shape[1]
@@ -397,16 +422,21 @@
     other = shifted(mine, "core", 1)
 
     core = lax.axis_index("core").astype(jnp.int32).reshape(1)
-    own, squares, send = gram_parts(core, mine, other)
-    across = lax.ppermute(send, ("side", "pair"), [(0, 3), (3, 0), (1, 2), (2, 1)])
-    count = own.shape[0]
+    own_a, own_b, squares, send_a, send_b = gram_parts(core, mine, other)
+    across_a = to_other_owner(send_a)
+    across_b = to_other_owner(send_b)
     width = coords // blocks
-    mine_later, other_later, _ = lax.optimization_barrier((mine, other, send))
+    mine_later, other_later, _ = lax.optimization_barrier((mine, other, across_a))
     rows = in_order(core, mine_later, other_later, width)
-    half = (own + across.astype(jnp.float32)).astype(jnp.bfloat16)
-    rest = shifted(half, "core", 1)
-    started = spread(core, half, width)
-    term = block_scores(coords, core, squares, across[count - 16 :], rest, started, mine, rows)
+    half_a = (own_a + across_a.astype(jnp.float32)).astype(jnp.bfloat16)
+    rest_a = shifted(half_a, "core", 1)
+    started = spread(core, half_a, rest_a, width)
+    across_b, rows = lax.optimization_barrier((across_b, rows))
+    half_b = (own_b + across_b.astype(jnp.float32)).astype(jnp.bfloat16)
+    rest_b = shifted(half_b, "core", 1)
+    started = spread_on(core, half_b, started)
+    far_squares = across_a[across_a.shape[0] - 16 :]
+    term = block_scores(coords, core, squares, far_squares, rest_b, started, mine, rows)
     terms = lax.all_to_all(term.reshape(blocks, examples, -1), OWNERS, 0, 0, tiled=True)
     scores = jnp.sum(terms.astype(jnp.float32), axis=0)
     return scores * float(examples * lax.axis_size(("side", "pair")))

time: 79.2 us -> 78.6 us (level)
  waiting for transfers between devices: 16.4 us -> 14.4 us
  starting transfers between devices: 2.07 us -> 3.49 us
    ppermute x1 -> x2, waiting for transfers between devices: 13.4 us -> 11.3 us  [to_other_owner(): lax.ppermute(value, ('side', 'pair'), [(0, 3), (3, 0), (1, 2), (2, 1)])]
    ppermute x1 -> x2, starting transfers between devices: 1.98 us -> 3.32 us  [to_other_owner(): lax.ppermute(value, ('side', 'pair'), [(0, 3), (3, 0), (1, 2), (2, 1)])]
    ppermute x2 -> x3, waiting for transfers between devices: 3.09 us -> 3.18 us  [shifted(): lax.ppermute(value, axis, [(i, (i + shift) % size) for i in range(size)])]
  transfers between devices with their start and end apart: 3 -> 5, of which waited for: 3 -> 4; matrix products, arithmetic and copies ran while one was open for 0% -> 0% of each run, Pallas kernels for 2% -> 2%
where the time goes in v5:
time: 78.6 us; the launch traced here: 78.4 us
  blocking collectives  43.6 us (55%)
  Pallas kernels  15.9 us (20%)
  waiting for transfers between devices  14.4 us (18%)
  starting transfers between devices  3.49 us (4%)
  other arithmetic  0.84 us (1%)
    all_to_all x1, blocking collectives, shards(): arrived = lax.all_to_all(by_block, OWNERS, 0, 0, tiled=True)  28.2 us
    all_to_all x1, blocking collectives, shards(): lax.all_to_all(term.reshape(blocks, examples, -1), OWNERS, 0, 0, tiled=True)  15.4 us
    ppermute x2, waiting for transfers between devices, to_other_owner(): lax.ppermute(value, ('side', 'pair'), [(0, 3), (3, 0), (1, 2), (2, 1)])  11.3 us
    pallas_call x1, Pallas kernels, features_of(): pl.pallas_call(feature_kernel, grid=(steps,), in_specs=[pl.BlockSpec(memo...  8.04 us
    pallas_call x1, Pallas kernels, block_scores(): pl.pallas_call(functools.partial(solve_kernel, coords), in_specs=[smem] +...  5.49 us
    ppermute x2, starting transfers between devices, to_other_owner(): lax.ppermute(value, ('side', 'pair'), [(0, 3), (3, 0), (1, 2), (2, 1)])  3.32 us
    ppermute x3, waiting for transfers between devices, shifted(): lax.ppermute(value, axis, [(i, (i + shift) % size) for i in range(size)])  3.18 us
  transfers between devices with their start and end apart: 5, of which 4 were waited for; matrix products, arithmetic and copies ran while one was open for 0% of the time, Pallas kernels for 2%

profile of v5, /device:TPU:0, one launch (start us, length us, event | category | flops | bytes accessed | tf_op | source)
XLA Modules:
  0.0 78.4 jit_solution(6577960565749271173)
XLA Ops:
  0.0 8.0 %features.1 = bf16[32,16,1152]{2,1,0:T(8,128)(2,1)S(1)} custom-call(s32[1]{0:T(128)} %bitcast.1.side_ref, bf16[1024,3072]{1,0:T(8,128)(2,1)} %act_ref.1, bf16[1024,3072]{1,0:T(8,128)(2,1)} %grad_ref.1, bf16[3072,128]{1,0:T(8,128)(2,1)} %pa_ref.1, bf16[3072,256]{1,0:T(8,128)(2,1)} %po_ref.1), custom_call_target="tpu_custom_call" | custom-call | tf_op jit(solution)/shard_map/features/pallas_call | solution.py:90
  8.1 28.2 %all_to_all.10 = bf16[32,16,1152]{2,1,0:T(8,128)(2,1)S(1)} all-to-all(bf16[32,16,1152]{2,1,0:T(8,128)(2,1)S(1)} %features.1), channel_id=1, replica_groups=mesh['side'=2,'pair'=2,'blk_0'=4,'blk_1'=4,'core'=2] {'pair','blk_0','bl..., dimensions={0} | all-to-all | bytes 2359296 | tf_op jit(solution)/shard_map/all_to_all | solution.py:420
  36.3 0.0 collective-permute-start
  36.3 0.6 own_gram.1.acc_ref
  36.9 2.3 %collective-permute-done.other_ref = bf16[512,1152]{1,0:T(8,128)(2,1)S(1)} collective-permute-done((bf16[512,1152]{1,0:T(8,128)(2,1)S(1)}, bf16[512,1152]{1,0:T(8,128)(2,1)S(1)}, u32[]{:S(2)}, u32[]{:S(2)}) %collective-permute-start) | collective-permute-done | bytes 1179680 | tf_op jit(solution)/shard_map/ppermute | solution.py:407
  39.1 0.6 gram_parts.1
  39.7 2.0 %collective-permute-start.1 = (bf16[1040,128]{1,0:T(8,128)(2,1)S(1)}, bf16[1040,128]{1,0:T(8,128)(2,1)S(1)}, u32[]{:S(2)}, u32[]{:S(2)}) collective-permute-start(bf16[1040,128]{1,0:T(8,128)(2,1)S(1)} %get-tuple-element.16), channel_id=1, source_target_pairs={{0,96},{96,0},{32,64},{64,32},{1,97},{97,1},{33,65},{65,33},{2,98}... | collective-permute-start | bytes 798728 | tf_op jit(solution)/shard_map/ppermute | solution.py:411
  41.7 1.3 %collective-permute-start.2 = (bf16[1040,128]{1,0:T(8,128)(2,1)S(1)}, bf16[1040,128]{1,0:T(8,128)(2,1)S(1)}, u32[]{:S(2)}, u32[]{:S(2)}) collective-permute-start(bf16[1040,128]{1,0:T(8,128)(2,1)S(1)} %get-tuple-element.18), channel_id=1, source_target_pairs={{0,96},{96,0},{32,64},{64,32},{1,97},{97,1},{33,65},{65,33},{2,98}... | collective-permute-start | bytes 798728 | tf_op jit(solution)/shard_map/ppermute | solution.py:411
  43.0 7.2 %collective-permute-done.1 = bf16[1040,128]{1,0:T(8,128)(2,1)S(1)} collective-permute-done((bf16[1040,128]{1,0:T(8,128)(2,1)S(1)}, bf16[1040,128]{1,0:T(8,128)(2,1)S(1)}, u32[]{:S(2)}, u32[]{:S(2)}) %collective-permute-start.1) | collective-permute-done | bytes 266272 | tf_op jit(solution)/shard_map/ppermute | solution.py:411
  50.2 0.1 add_convert_fusion.half_ref
  50.3 0.1 collective-permute-start.4
  50.4 0.7 in_order.1.group_ref
  51.1 4.0 %collective-permute-done.2 = bf16[1040,128]{1,0:T(8,128)(2,1)S(1)} collective-permute-done((bf16[1040,128]{1,0:T(8,128)(2,1)S(1)}, bf16[1040,128]{1,0:T(8,128)(2,1)S(1)}, u32[]{:S(2)}, u32[]{:S(2)}) %collective-permute-start.2) | collective-permute-done | bytes 266272 | tf_op jit(solution)/shard_map/ppermute | solution.py:411
  55.1 0.1 add_convert_fusion.1.half_ref
  55.2 0.1 collective-permute-start.3
  55.3 0.0 collective-permute-done.4.rest_ref
  55.3 0.4 spread.1.started_ref
  55.7 0.2 spread_on.1.started_ref
  55.9 0.9 %collective-permute-done.3.rest_ref = bf16[1040,128]{1,0:T(8,128)(2,1)S(1)} collective-permute-done((bf16[1040,128]{1,0:T(8,128)(2,1)S(1)}, bf16[1040,128]{1,0:T(8,128)(2,1)S(1)}, u32[]{:S(2)}, u32[]{:S(2)}) %collective-permute-start.3) | collective-permute-done | bytes 266272 | tf_op jit(solution)/shard_map/ppermute | solution.py:407
  56.8 5.5 %solve.1 = (bf16[512,512]{1,0:T(8,128)(2,1)S(1)}, bf16[1024,1024]{1,0:T(8,128)(2,1)S(1)}) custom-call(s32[1]{0:T(128)} %bitcast.core_ref, f32[8,128]{1,0:T(8,128)S(1)} %get-tuple-element.15.sum_ref, bf16[16,128]{1,0:T(8,128)(2,1)S(1)} %slice.9.far_sum_ref, bf16[1040,128]{1,0:T(8,128)(2,1)S(1)} %collective-permute-done.3.rest_ref, ...), custom_call_target="tpu_custom_call", output_to_operand_aliasing={{1}: (4, {})} | custom-call | tf_op jit(solution)/shard_map/solve/pallas_call | solution.py:386
  62.3 15.4 %all_to_all.11 = bf16[32,16,512]{2,1,0:T(8,128)(2,1)S(1)} all-to-all(bf16[32,16,512]{2,1,0:T(8,128)(2,1)S(1)} %bitcast.9), channel_id=1, replica_groups=mesh['side'=2,'pair'=2,'blk_0'=4,'blk_1'=4,'core'=2] {'pair','blk_0','bl..., dimensions={0} | all-to-all | bytes 1048576 | tf_op jit(solution)/shard_map/all_to_all | solution.py:440
  77.7 0.1 convert_reduce_fusion
  77.8 0.6 broadcast_multiply_fusion
  (2 shorter events, 0.0 us)
Async XLA Ops:
  36.3 2.8 %collective-permute-start = (bf16[512,1152]{1,0:T(8,128)(2,1)S(1)}, bf16[512,1152]{1,0:T(8,128)(2,1)S(1)}, u32[]{:S(2)}, u32[]{:S(2)}) collective-permute-start(bf16[512,1152]{1,0:T(8,128)(2,1)S(1)} %bitcast.4), channel_id=1, source_target_pairs={{0,1},{1,0},{2,3},{3,2},{4,5},{5,4},{6,7},{7,6},{8,9},{9,8},{10,11... | collective-permute-start | bytes 3538952 | tf_op jit(solution)/shard_map/ppermute | solution.py:407
  39.7 10.5 %collective-permute-start.1 = (bf16[1040,128]{1,0:T(8,128)(2,1)S(1)}, bf16[1040,128]{1,0:T(8,128)(2,1)S(1)}, u32[]{:S(2)}, u32[]{:S(2)}) collective-permute-start(bf16[1040,128]{1,0:T(8,128)(2,1)S(1)} %get-tuple-element.16), channel_id=1, source_target_pairs={{0,96},{96,0},{32,64},{64,32},{1,97},{97,1},{33,65},{65,33},{2,98}... | collective-permute-start | bytes 798728 | tf_op jit(solution)/shard_map/ppermute | solution.py:411
  41.7 13.4 %collective-permute-start.2 = (bf16[1040,128]{1,0:T(8,128)(2,1)S(1)}, bf16[1040,128]{1,0:T(8,128)(2,1)S(1)}, u32[]{:S(2)}, u32[]{:S(2)}) collective-permute-start(bf16[1040,128]{1,0:T(8,128)(2,1)S(1)} %get-tuple-element.18), channel_id=1, source_target_pairs={{0,96},{96,0},{32,64},{64,32},{1,97},{97,1},{33,65},{65,33},{2,98}... | collective-permute-start | bytes 798728 | tf_op jit(solution)/shard_map/ppermute | solution.py:411
  50.3 5.0 %collective-permute-start.4 = (bf16[1040,128]{1,0:T(8,128)(2,1)S(1)}, bf16[1040,128]{1,0:T(8,128)(2,1)S(1)}, u32[]{:S(2)}, u32[]{:S(2)}) collective-permute-start(bf16[1040,128]{1,0:T(8,128)(2,1)S(1)} %add_convert_fusion.half_ref), channel_id=1, source_target_pairs={{0,1},{1,0},{2,3},{3,2},{4,5},{5,4},{6,7},{7,6},{8,9},{9,8},{10,11... | collective-permute-start | bytes 798728 | tf_op jit(solution)/shard_map/ppermute | solution.py:407
  55.2 1.6 %collective-permute-start.3 = (bf16[1040,128]{1,0:T(8,128)(2,1)S(1)}, bf16[1040,128]{1,0:T(8,128)(2,1)S(1)}, u32[]{:S(2)}, u32[]{:S(2)}) collective-permute-start(bf16[1040,128]{1,0:T(8,128)(2,1)S(1)} %add_convert_fusion.1.half_ref), channel_id=1, source_target_pairs={{0,1},{1,0},{2,3},{3,2},{4,5},{5,4},{6,7},{7,6},{8,9},{9,8},{10,11... | collective-permute-start | bytes 798728 | tf_op jit(solution)/shard_map/ppermute | solution.py:407

commit v6 on v4

--- a/solution.py
+++ b/solution.py
@@ -35,7 +35,7 @@
 
 
 def feature_kernel(
-    side_ref, act_ref, grad_ref, pa_ref, po_ref, out_ref, act_low, grad_low, feats, by_coord
+    side_ref, act_ref, grad_ref, pa_ref, po_ref, out_ref, sum_ref, act_low, grad_low, feats, by_coord
 ):
     step = pl.program_id(0)
     steps = pl.num_programs(0)
@@ -67,16 +67,14 @@
         turn = side_ref[0] * (blocks // 2)
         for k in range(blocks):
             low = by_coord[k].astype(jnp.bfloat16)
-            out_ref[lax.rem(k + turn, blocks), :, :width] = low
+            out_ref[lax.rem(k + turn, blocks)] = low
             wide = low.astype(jnp.float32)
             acc = acc + wide * wide
         part = jnp.zeros((8, TILE), jnp.float32)
         for r in range(0, examples, 8):
             for c in range(0, width, TILE):
                 part = part + acc[r : r + 8, c : c + TILE]
-        tail = as_three(jnp.sum(part, axis=0, keepdims=True))
-        for k in range(blocks):
-            out_ref[k, :, width:] = tail
+        sum_ref[...] = part
 
 
 def features_of(side, activations, out_grads, proj_act, proj_out, blocks):
@@ -97,8 +95,14 @@
             pl.BlockSpec((depth, ra), lambda i: (0, 0), pipeline_mode=pl.Buffered(1)),
             pl.BlockSpec((depth, rb), lambda i: (0, 0), pipeline_mode=pl.Buffered(1)),
         ],
-        out_specs=pl.BlockSpec((blocks, examples, width + TILE), lambda i: (0, 0, 0)),
-        out_shape=jax.ShapeDtypeStruct((blocks, examples, width + TILE), jnp.bfloat16),
+        out_specs=[
+            pl.BlockSpec((blocks, examples, width), lambda i: (0, 0, 0)),
+            pl.BlockSpec((8, TILE), lambda i: (0, 0)),
+        ],
+        out_shape=[
+            jax.ShapeDtypeStruct((blocks, examples, width), jnp.bfloat16),
+            jax.ShapeDtypeStruct((8, TILE), jnp.float32),
+        ],
         scratch_shapes=[
             pltpu.VMEM((tokens, ra), jnp.bfloat16),
             pltpu.VMEM((tokens, rb), jnp.bfloat16),
@@ -148,14 +152,7 @@
         acc_ref[part_of(n, m), :] = value
 
 
-def gram_kernel(core_ref, acc_ref, mine_sum_ref, other_ref, own_ref, sum_ref, send_ref):
-    width = other_ref.shape[1] - TILE
-    squares = jnp.sum(
-        mine_sum_ref[...].astype(jnp.float32) + other_ref[:, width:].astype(jnp.float32),
-        axis=0,
-        keepdims=True,
-    )
-    sum_ref[...] = jnp.broadcast_to(squares, sum_ref.shape)
+def gram_kernel(core_ref, acc_ref, other_ref, own_ref, send_ref):
     row, column = row_and_column()
     parts = {}
     for n, m, value in gram_products(core_ref[0], other_ref):
@@ -183,7 +180,7 @@
     last = jnp.where(turn == 3, diagonals[0], jnp.where(turn == 4, diagonals[1], 0.0))
     rows = slice(2 * PIECES * TILE, 2 * PIECES * TILE + 16)
     own_ref[rows, :] = last
-    send_ref[rows, :] = as_three(squares) + last.astype(jnp.bfloat16)
+    send_ref[rows, :] = last.astype(jnp.bfloat16)
 
 
 def gram_parts(core, mine, other):
@@ -201,16 +198,15 @@
     )(core, mine)
     return pl.pallas_call(
         gram_kernel,
-        in_specs=[smem, vmem, vmem, vmem],
-        out_specs=[vmem, vmem, vmem],
+        in_specs=[smem, vmem, vmem],
+        out_specs=[vmem, vmem],
         out_shape=[
             jax.ShapeDtypeStruct((count, TILE), jnp.float32),
-            jax.ShapeDtypeStruct((8, TILE), jnp.float32),
             jax.ShapeDtypeStruct((count, TILE), jnp.bfloat16),
         ],
         compiler_params=params,
         name="gram_parts",
-    )(core, acc, mine[:, mine.shape[1] - TILE :], other)
+    )(core, acc, other)
 
 
 def put_pieces(half, ref, gram):
@@ -258,7 +254,7 @@
             at = slice((g * count + p) * piece, (g * count + p + 1) * piece)
             for which, ref in ((core, mine_ref), (1 - core, other_ref)):
                 to = pl.multiple_of(p * 2 * piece + which * piece, piece)
-                ordered[g, pl.ds(to, piece), :] = ref[at, :width]
+                ordered[g, pl.ds(to, piece), :] = ref[at, :]
         out_ref[g] = ordered[g].T
 
 
@@ -280,7 +276,6 @@
     coords,
     core_ref,
     sum_ref,
-    far_sum_ref,
     rest_ref,
     started_ref,
     mine_ref,
@@ -306,11 +301,7 @@
         image = jnp.sum(image, axis=0, keepdims=True)
         radius = jnp.sqrt(jnp.sum(image * image, axis=1, keepdims=True) + 1e-06)
         vector = image / radius
-    total = jnp.sum(sum_ref[0:1, :], axis=1, keepdims=True) + jnp.sum(
-        jnp.sum(far_sum_ref[...].astype(jnp.float32)[0:3, :], axis=0, keepdims=True),
-        axis=1,
-        keepdims=True,
-    )
+    total = jnp.sum(jnp.sum(sum_ref[...], axis=0, keepdims=True), axis=1, keepdims=True)
     damping = damping_rate * (total / coords)
     center = damping + radius
     strides = [1.0 / center]
@@ -331,7 +322,7 @@
     def right_side(at):
         return mine_ref[:, at].astype(jnp.float32)
 
-    for at, value in operate(lambda: mine_ref[:, :width]):
+    for at, value in operate(lambda: mine_ref[...]):
         value = keep[0] * right_side(at) - strides[0] * value
         first[:, at] = value
         low[0, :, at] = value.astype(jnp.bfloat16)
@@ -356,7 +347,7 @@
         ).astype(out_ref.dtype)
 
 
-def block_scores(coords, core, squares, far_squares, rest, started, mine, rows):
+def block_scores(coords, core, squares, rest, started, mine, rows):
     vmem = pl.BlockSpec(memory_space=pltpu.VMEM)
     smem = pl.BlockSpec(memory_space=pltpu.SMEM)
     examples = mine.shape[0]
@@ -364,7 +355,7 @@
     field = (examples, width)
     return pl.pallas_call(
         functools.partial(solve_kernel, coords),
-        in_specs=[smem] + [vmem] * 6,
+        in_specs=[smem] + [vmem] * 5,
         out_specs=[vmem, vmem],
         out_shape=[
             jax.ShapeDtypeStruct((examples, examples), jnp.bfloat16),
@@ -375,15 +366,19 @@
             pltpu.VMEM(field, jnp.float32),
             pltpu.VMEM((2,) + field, jnp.bfloat16),
         ],
-        input_output_aliases={4: 1},
+        input_output_aliases={3: 1},
         compiler_params=pltpu.CompilerParams(vmem_limit_bytes=32 << 20),
         name="solve",
-    )(core, squares, far_squares, rest, started, mine, rows)[0]
+    )(core, squares, rest, started, mine, rows)[0]
 
 
 def shifted(value, axis, shift):
     size = lax.axis_size(axis)
     return lax.ppermute(value, axis, [(i, (i + shift) % size) for i in range(size)])
+
+
+def to_other_owner(value):
+    return lax.ppermute(value, ("side", "pair"), [(0, 3), (3, 0), (1, 2), (2, 1)])
 
 
 def shards(activations, out_grads, proj_act, proj_out):
@@ -391,22 +386,29 @@
     coords = proj_act.shape[1] * proj_out.shape[1]
     blocks = lax.axis_size(OWNERS)
     side = lax.axis_index("side").astype(jnp.int32).reshape(1)
-    by_block = features_of(side, activations, out_grads, proj_act, proj_out, blocks)
+    by_block, squares = features_of(side, activations, out_grads, proj_act, proj_out, blocks)
     arrived = lax.all_to_all(by_block, OWNERS, 0, 0, tiled=True)
     mine = arrived.reshape(blocks * examples, -1)
     other = shifted(mine, "core", 1)
 
     core = lax.axis_index("core").astype(jnp.int32).reshape(1)
-    own, squares, send = gram_parts(core, mine, other)
-    across = lax.ppermute(send, ("side", "pair"), [(0, 3), (3, 0), (1, 2), (2, 1)])
-    count = own.shape[0]
+    own, send = gram_parts(core, mine, other)
+    squares = squares + to_other_owner(squares)
+    squares, send, mine_later, other_later = lax.optimization_barrier(
+        (squares, send, mine, other)
+    )
+    across = to_other_owner(send)
     width = coords // blocks
-    mine_later, other_later, _ = lax.optimization_barrier((mine, other, send))
+    squares = jnp.broadcast_to(squares, (blocks,) + squares.shape)
+    squares = lax.all_to_all(squares, OWNERS, 0, 0, tiled=True)
+    across, squares = lax.optimization_barrier((across, squares))
     rows = in_order(core, mine_later, other_later, width)
     half = (own + across.astype(jnp.float32)).astype(jnp.bfloat16)
+    squares = jnp.sum(squares, axis=0)
     rest = shifted(half, "core", 1)
+    squares = squares + shifted(squares, "core", 1)
     started = spread(core, half, width)
-    term = block_scores(coords, core, squares, across[count - 16 :], rest, started, mine, rows)
+    term = block_scores(coords, core, squares, rest, started, mine, rows)
     terms = lax.all_to_all(term.reshape(blocks, examples, -1), OWNERS, 0, 0, tiled=True)
     scores = jnp.sum(terms.astype(jnp.float32), axis=0)
     return scores * float(examples * lax.axis_size(("side", "pair")))

time: 79.2 us -> 79.6 us (level)
  waiting for transfers between devices: 16.4 us -> 2.29 us
  blocking collectives: 43.6 us -> 53.6 us
  starting transfers between devices: 2.07 us -> 6.29 us
    all_to_all x0 -> x1, blocking collectives: none -> 12.5 us  [shards(): squares = lax.all_to_all(squares, OWNERS, 0, 0, tiled=True)]
    ppermute x1 -> x2, waiting for transfers between devices: 13.4 us -> 2.04 us  [to_other_owner(): lax.ppermute(value, ('side', 'pair'), [(0, 3), (3, 0), (1, 2), (2, 1)])]
    ppermute x1 -> x2, starting transfers between devices: 1.98 us -> 5.63 us  [to_other_owner(): lax.ppermute(value, ('side', 'pair'), [(0, 3), (3, 0), (1, 2), (2, 1)])]
    ppermute x2 -> x3, waiting for transfers between devices: 3.09 us -> 0.25 us  [shifted(): lax.ppermute(value, axis, [(i, (i + shift) % size) for i in range(size)])]
    all_to_all x1, blocking collectives: 28.2 us -> 25.7 us  [shards(): arrived = lax.all_to_all(by_block, OWNERS, 0, 0, tiled=True)]
  transfers between devices with their start and end apart: 3 -> 5, of which waited for: 3 -> 2; matrix products, arithmetic and copies ran while one was open for 0% -> 0% of each run, Pallas kernels for 2% -> 2%
where the time goes in v6:
time: 79.6 us; the launch traced here: 79.2 us
  blocking collectives  53.6 us (67%)
  Pallas kernels  16.1 us (20%)
  starting transfers between devices  6.29 us (8%)
  waiting for transfers between devices  2.29 us (3%)
  other arithmetic  0.89 us (1%)
    all_to_all x1, blocking collectives, shards(): arrived = lax.all_to_all(by_block, OWNERS, 0, 0, tiled=True)  25.7 us
    all_to_all x1, blocking collectives, shards(): lax.all_to_all(term.reshape(blocks, examples, -1), OWNERS, 0, 0, tiled=True)  15.4 us
    all_to_all x1, blocking collectives, shards(): squares = lax.all_to_all(squares, OWNERS, 0, 0, tiled=True)  12.5 us
    pallas_call x1, Pallas kernels, features_of(): pl.pallas_call(feature_kernel, grid=(steps,), in_specs=[pl.BlockSpec(memo...  8.01 us
    pallas_call x1, Pallas kernels, block_scores(): pl.pallas_call(functools.partial(solve_kernel, coords), in_specs=[smem] +...  5.87 us
    ppermute x2, starting transfers between devices, to_other_owner(): lax.ppermute(value, ('side', 'pair'), [(0, 3), (3, 0), (1, 2), (2, 1)])  5.63 us
    ppermute x2, waiting for transfers between devices, to_other_owner(): lax.ppermute(value, ('side', 'pair'), [(0, 3), (3, 0), (1, 2), (2, 1)])  2.04 us
  transfers between devices with their start and end apart: 5, of which 2 were waited for; matrix products, arithmetic and copies ran while one was open for 0% of the time, Pallas kernels for 2%

profile of v6, /device:TPU:0, one launch (start us, length us, event | category | flops | bytes accessed | tf_op | source)
XLA Modules:
  0.0 79.2 jit_solution(4342309201460831510)
XLA Ops:
  0.0 8.0 %features.1 = (bf16[32,16,1024]{2,1,0:T(8,128)(2,1)S(1)}, f32[8,128]{1,0:T(8,128)S(1)}) custom-call(s32[1]{0:T(128)} %bitcast.1.side_ref, bf16[1024,3072]{1,0:T(8,128)(2,1)} %act_ref.1, bf16[1024,3072]{1,0:T(8,128)(2,1)} %grad_ref.1, bf16[3072,128]{1,0:T(8,128)(2,1)} %pa_ref.1, bf16[3072,256]{1,0:T(8,128)(2,1)} %po_ref.1), custom_call_target="tpu_custom_call" | custom-call | tf_op jit(solution)/shard_map/features/pallas_call | solution.py:88
  8.0 25.7 %all_to_all.15 = bf16[32,16,1024]{2,1,0:T(8,128)(2,1)S(1)} all-to-all(bf16[32,16,1024]{2,1,0:T(8,128)(2,1)S(1)} %get-tuple-element.17), channel_id=1, replica_groups=mesh['side'=2,'pair'=2,'blk_0'=4,'blk_1'=4,'core'=2] {'pair','blk_0','bl..., dimensions={0} | all-to-all | bytes 2097152 | tf_op jit(solution)/shard_map/all_to_all | solution.py:390
  33.7 0.0 collective-permute-start.1
  33.7 2.8 %collective-permute-start = (f32[8,128]{1,0:T(8,128)S(1)}, f32[8,128]{1,0:T(8,128)S(1)}, u32[]{:S(2)}, u32[]{:S(2)}) collective-permute-start(f32[8,128]{1,0:T(8,128)S(1)} %get-tuple-element.16), channel_id=1, source_target_pairs={{0,96},{96,0},{32,64},{64,32},{1,97},{97,1},{33,65},{65,33},{2,98}... | collective-permute-start | bytes 12296 | tf_op jit(solution)/shard_map/ppermute | solution.py:381
  36.5 2.0 %collective-permute-done = f32[8,128]{1,0:T(8,128)S(1)} collective-permute-done((f32[8,128]{1,0:T(8,128)S(1)}, f32[8,128]{1,0:T(8,128)S(1)}, u32[]{:S(2)}, u32[]{:S(2)}) %collective-permute-start) | collective-permute-done | bytes 4128 | tf_op jit(solution)/shard_map/ppermute | solution.py:381
  38.5 0.6 own_gram.1.acc_ref
  39.1 0.0 collective-permute-done.1.other_ref
  39.1 0.6 gram_parts.1
  39.7 2.9 %collective-permute-start.2 = (bf16[2064,128]{1,0:T(8,128)(2,1)S(1)}, bf16[2064,128]{1,0:T(8,128)(2,1)S(1)}, u32[]{:S(2)}, u32[]{:S(2)}) collective-permute-start(bf16[2064,128]{1,0:T(8,128)(2,1)S(1)} %get-tuple-element.19), channel_id=1, source_target_pairs={{0,96},{96,0},{32,64},{64,32},{1,97},{97,1},{33,65},{65,33},{2,98}... | collective-permute-start | bytes 1585160 | tf_op jit(solution)/shard_map/ppermute | solution.py:381
  42.6 12.5 %all_to_all.16 = f32[32,8,128]{2,1,0:T(8,128)S(1)} all-to-all(f32[32,8,128]{2,1,0:T(8,128)S(1)} %broadcast_in_dim.3), channel_id=1, replica_groups=mesh['side'=2,'pair'=2,'blk_0'=4,'blk_1'=4,'core'=2] {'pair','blk_0','bl..., dimensions={0} | all-to-all | bytes 262144 | tf_op jit(solution)/shard_map/all_to_all | solution.py:403
  55.0 0.0 collective-permute-done.2
  55.0 0.1 add_convert_fusion.half_ref
  55.2 0.1 collective-permute-start.4
  55.3 0.6 collective-permute-start.3
  55.9 0.7 in_order.1.group_ref
  56.6 0.4 spread.1.started_ref
  56.9 0.2 collective-permute-done.3
  57.2 0.0 collective-permute-done.4.rest_ref
  57.2 5.9 %solve.1 = (bf16[512,512]{1,0:T(8,128)(2,1)S(1)}, bf16[1024,1024]{1,0:T(8,128)(2,1)S(1)}) custom-call(s32[1]{0:T(128)} %bitcast.core_ref, f32[8,128]{1,0:T(8,128)S(1)} %add.10.sum_ref, bf16[2064,128]{1,0:T(8,128)(2,1)S(1)} %collective-permute-done.4.rest_ref, bf16[1024,1024]{1,0:T(8,128)(2,1)S(1)} %spread.1.started_ref, ...), custom_call_target="tpu_custom_call", output_to_operand_aliasing={{1}: (3, {})} | custom-call | tf_op jit(solution)/shard_map/solve/pallas_call | solution.py:356
  63.1 15.4 %all_to_all.17 = bf16[32,16,512]{2,1,0:T(8,128)(2,1)S(1)} all-to-all(bf16[32,16,512]{2,1,0:T(8,128)(2,1)S(1)} %bitcast.8), channel_id=1, replica_groups=mesh['side'=2,'pair'=2,'blk_0'=4,'blk_1'=4,'core'=2] {'pair','blk_0','bl..., dimensions={0} | all-to-all | bytes 1048576 | tf_op jit(solution)/shard_map/all_to_all | solution.py:412
  78.5 0.1 convert_reduce_fusion
  78.6 0.6 broadcast_multiply_fusion
  (4 shorter events, 0.1 us)
Async XLA Ops:
  33.7 5.4 %collective-permute-start.1 = (bf16[512,1024]{1,0:T(8,128)(2,1)S(1)}, bf16[512,1024]{1,0:T(8,128)(2,1)S(1)}, u32[]{:S(2)}, u32[]{:S(2)}) collective-permute-start(bf16[512,1024]{1,0:T(8,128)(2,1)S(1)} %bitcast.4), channel_id=1, source_target_pairs={{0,1},{1,0},{2,3},{3,2},{4,5},{5,4},{6,7},{7,6},{8,9},{9,8},{10,11... | collective-permute-start | bytes 3145736 | tf_op jit(solution)/shard_map/ppermute | solution.py:377
  33.7 4.8 %collective-permute-start = (f32[8,128]{1,0:T(8,128)S(1)}, f32[8,128]{1,0:T(8,128)S(1)}, u32[]{:S(2)}, u32[]{:S(2)}) collective-permute-start(f32[8,128]{1,0:T(8,128)S(1)} %get-tuple-element.16), channel_id=1, source_target_pairs={{0,96},{96,0},{32,64},{64,32},{1,97},{97,1},{33,65},{65,33},{2,98}... | collective-permute-start | bytes 12296 | tf_op jit(solution)/shard_map/ppermute | solution.py:381
  39.7 15.3 %collective-permute-start.2 = (bf16[2064,128]{1,0:T(8,128)(2,1)S(1)}, bf16[2064,128]{1,0:T(8,128)(2,1)S(1)}, u32[]{:S(2)}, u32[]{:S(2)}) collective-permute-start(bf16[2064,128]{1,0:T(8,128)(2,1)S(1)} %get-tuple-element.19), channel_id=1, source_target_pairs={{0,96},{96,0},{32,64},{64,32},{1,97},{97,1},{33,65},{65,33},{2,98}... | collective-permute-start | bytes 1585160 | tf_op jit(solution)/shard_map/ppermute | solution.py:381
  55.2 2.0 %collective-permute-start.4 = (bf16[2064,128]{1,0:T(8,128)(2,1)S(1)}, bf16[2064,128]{1,0:T(8,128)(2,1)S(1)}, u32[]{:S(2)}, u32[]{:S(2)}) collective-permute-start(bf16[2064,128]{1,0:T(8,128)(2,1)S(1)} %add_convert_fusion.half_ref), channel_id=1, source_target_pairs={{0,1},{1,0},{2,3},{3,2},{4,5},{5,4},{6,7},{7,6},{8,9},{9,8},{10,11... | collective-permute-start | bytes 1585160 | tf_op jit(solution)/shard_map/ppermute | solution.py:377
  55.3 1.9 %collective-permute-start.3 = (f32[8,128]{1,0:T(8,128)S(1)}, f32[8,128]{1,0:T(8,128)S(1)}, u32[]{:S(2)}, u32[]{:S(2)}) collective-permute-start(f32[8,128]{1,0:T(8,128)S(1)} %reduce_sum.18), channel_id=1, source_target_pairs={{0,1},{1,0},{2,3},{3,2},{4,5},{5,4},{6,7},{7,6},{8,9},{9,8},{10,11... | collective-permute-start | bytes 12296 | tf_op jit(solution)/shard_map/ppermute | solution.py:377

commit v7 on v6

--- a/solution.py
+++ b/solution.py
@@ -393,7 +393,7 @@
 
     core = lax.axis_index("core").astype(jnp.int32).reshape(1)
     own, send = gram_parts(core, mine, other)
-    squares = squares + to_other_owner(squares)
+    squares = squares + shifted(squares, "core", 1)
     squares, send, mine_later, other_later = lax.optimization_barrier(
         (squares, send, mine, other)
     )
@@ -406,7 +406,7 @@
     half = (own + across.astype(jnp.float32)).astype(jnp.bfloat16)
     squares = jnp.sum(squares, axis=0)
     rest = shifted(half, "core", 1)
-    squares = squares + shifted(squares, "core", 1)
+    squares = squares + to_other_owner(squares)
     started = spread(core, half, width)
     term = block_scores(coords, core, squares, rest, started, mine, rows)
     terms = lax.all_to_all(term.reshape(blocks, examples, -1), OWNERS, 0, 0, tiled=True)

time: 79.6 us -> 80.4 us (1.010)
  waiting for transfers between devices: 2.29 us -> 3.14 us
    ppermute x3, waiting for transfers between devices: 0.25 us -> 2.16 us  [shifted(): lax.ppermute(value, axis, [(i, (i + shift) % size) for i in range(size)])]
    ppermute x2, waiting for transfers between devices: 2.04 us -> 0.98 us  [to_other_owner(): lax.ppermute(value, ('side', 'pair'), [(0, 3), (3, 0), (1, 2), (2, 1)])]
where the time goes in v7:
time: 80.4 us; the launch traced here: 79.8 us
  blocking collectives  53.3 us (66%)
  Pallas kernels  16.1 us (20%)
  starting transfers between devices  6.31 us (8%)
  waiting for transfers between devices  3.14 us (4%)
  other arithmetic  0.89 us (1%)
    all_to_all x1, blocking collectives, shards(): arrived = lax.all_to_all(by_block, OWNERS, 0, 0, tiled=True)  25.7 us
    all_to_all x1, blocking collectives, shards(): lax.all_to_all(term.reshape(blocks, examples, -1), OWNERS, 0, 0, tiled=True)  15.2 us
    all_to_all x1, blocking collectives, shards(): squares = lax.all_to_all(squares, OWNERS, 0, 0, tiled=True)  12.5 us
    pallas_call x1, Pallas kernels, features_of(): pl.pallas_call(feature_kernel, grid=(steps,), in_specs=[pl.BlockSpec(memo...  8.01 us
    pallas_call x1, Pallas kernels, block_scores(): pl.pallas_call(functools.partial(solve_kernel, coords), in_specs=[smem] +...  5.88 us
    ppermute x2, starting transfers between devices, to_other_owner(): lax.ppermute(value, ('side', 'pair'), [(0, 3), (3, 0), (1, 2), (2, 1)])  5.72 us
    ppermute x3, waiting for transfers between devices, shifted(): lax.ppermute(value, axis, [(i, (i + shift) % size) for i in range(size)])  2.16 us
  transfers between devices with their start and end apart: 5, of which 2 were waited for; matrix products, arithmetic and copies ran while one was open for 0% of the time, Pallas kernels for 2%

profile of v7, /device:TPU:0, one launch (start us, length us, event | category | flops | bytes accessed | tf_op | source)
XLA Modules:
  0.0 79.8 jit_solution(10794515171761698266)
XLA Ops:
  0.0 8.0 %features.1 = (bf16[32,16,1024]{2,1,0:T(8,128)(2,1)S(1)}, f32[8,128]{1,0:T(8,128)S(1)}) custom-call(s32[1]{0:T(128)} %bitcast.1.side_ref, bf16[1024,3072]{1,0:T(8,128)(2,1)} %act_ref.1, bf16[1024,3072]{1,0:T(8,128)(2,1)} %grad_ref.1, bf16[3072,128]{1,0:T(8,128)(2,1)} %pa_ref.1, bf16[3072,256]{1,0:T(8,128)(2,1)} %po_ref.1), custom_call_target="tpu_custom_call" | custom-call | tf_op jit(solution)/shard_map/features/pallas_call | solution.py:88
  8.0 25.7 %all_to_all.15 = bf16[32,16,1024]{2,1,0:T(8,128)(2,1)S(1)} all-to-all(bf16[32,16,1024]{2,1,0:T(8,128)(2,1)S(1)} %get-tuple-element.17), channel_id=1, replica_groups=mesh['side'=2,'pair'=2,'blk_0'=4,'blk_1'=4,'core'=2] {'pair','blk_0','bl..., dimensions={0} | all-to-all | bytes 2097152 | tf_op jit(solution)/shard_map/all_to_all | solution.py:390
  33.7 0.0 collective-permute-start.1
  33.7 0.5 collective-permute-start
  34.2 2.2 %collective-permute-done = f32[8,128]{1,0:T(8,128)S(1)} collective-permute-done((f32[8,128]{1,0:T(8,128)S(1)}, f32[8,128]{1,0:T(8,128)S(1)}, u32[]{:S(2)}, u32[]{:S(2)}) %collective-permute-start) | collective-permute-done | bytes 4128 | tf_op jit(solution)/shard_map/ppermute | solution.py:377
  36.4 0.6 own_gram.1.acc_ref
  36.9 0.0 collective-permute-done.1.other_ref
  37.0 0.6 gram_parts.1
  37.5 2.9 %collective-permute-start.2 = (bf16[2064,128]{1,0:T(8,128)(2,1)S(1)}, bf16[2064,128]{1,0:T(8,128)(2,1)S(1)}, u32[]{:S(2)}, u32[]{:S(2)}) collective-permute-start(bf16[2064,128]{1,0:T(8,128)(2,1)S(1)} %get-tuple-element.19), channel_id=1, source_target_pairs={{0,96},{96,0},{32,64},{64,32},{1,97},{97,1},{33,65},{65,33},{2,98}... | collective-permute-start | bytes 1585160 | tf_op jit(solution)/shard_map/ppermute | solution.py:381
  40.4 12.5 %all_to_all.16 = f32[32,8,128]{2,1,0:T(8,128)S(1)} all-to-all(f32[32,8,128]{2,1,0:T(8,128)S(1)} %broadcast_in_dim.3), channel_id=1, replica_groups=mesh['side'=2,'pair'=2,'blk_0'=4,'blk_1'=4,'core'=2] {'pair','blk_0','bl..., dimensions={0} | all-to-all | bytes 262144 | tf_op jit(solution)/shard_map/all_to_all | solution.py:403
  52.9 0.0 collective-permute-done.2
  52.9 0.1 add_convert_fusion.half_ref
  53.0 0.1 collective-permute-start.4
  53.1 2.9 %collective-permute-start.3 = (f32[8,128]{1,0:T(8,128)S(1)}, f32[8,128]{1,0:T(8,128)S(1)}, u32[]{:S(2)}, u32[]{:S(2)}) collective-permute-start(f32[8,128]{1,0:T(8,128)S(1)} %reduce_sum.18), channel_id=1, source_target_pairs={{0,96},{96,0},{32,64},{64,32},{1,97},{97,1},{33,65},{65,33},{2,98}... | collective-permute-start | bytes 12296 | tf_op jit(solution)/shard_map/ppermute | solution.py:381
  56.0 0.7 in_order.1.group_ref
  56.7 0.4 spread.1.started_ref
  57.1 1.0 %collective-permute-done.3 = f32[8,128]{1,0:T(8,128)S(1)} collective-permute-done((f32[8,128]{1,0:T(8,128)S(1)}, f32[8,128]{1,0:T(8,128)S(1)}, u32[]{:S(2)}, u32[]{:S(2)}) %collective-permute-start.3) | collective-permute-done | bytes 4128 | tf_op jit(solution)/shard_map/ppermute | solution.py:381
  58.0 0.0 collective-permute-done.4.rest_ref
  58.0 5.9 %solve.1 = (bf16[512,512]{1,0:T(8,128)(2,1)S(1)}, bf16[1024,1024]{1,0:T(8,128)(2,1)S(1)}) custom-call(s32[1]{0:T(128)} %bitcast.core_ref, f32[8,128]{1,0:T(8,128)S(1)} %add.10.sum_ref, bf16[2064,128]{1,0:T(8,128)(2,1)S(1)} %collective-permute-done.4.rest_ref, bf16[1024,1024]{1,0:T(8,128)(2,1)S(1)} %spread.1.started_ref, ...), custom_call_target="tpu_custom_call", output_to_operand_aliasing={{1}: (3, {})} | custom-call | tf_op jit(solution)/shard_map/solve/pallas_call | solution.py:356
  63.9 15.2 %all_to_all.17 = bf16[32,16,512]{2,1,0:T(8,128)(2,1)S(1)} all-to-all(bf16[32,16,512]{2,1,0:T(8,128)(2,1)S(1)} %bitcast.8), channel_id=1, replica_groups=mesh['side'=2,'pair'=2,'blk_0'=4,'blk_1'=4,'core'=2] {'pair','blk_0','bl..., dimensions={0} | all-to-all | bytes 1048576 | tf_op jit(solution)/shard_map/all_to_all | solution.py:412
  79.1 0.1 convert_reduce_fusion
  79.2 0.6 broadcast_multiply_fusion
  (4 shorter events, 0.1 us)
Async XLA Ops:
  33.7 3.3 %collective-permute-start.1 = (bf16[512,1024]{1,0:T(8,128)(2,1)S(1)}, bf16[512,1024]{1,0:T(8,128)(2,1)S(1)}, u32[]{:S(2)}, u32[]{:S(2)}) collective-permute-start(bf16[512,1024]{1,0:T(8,128)(2,1)S(1)} %bitcast.4), channel_id=1, source_target_pairs={{0,1},{1,0},{2,3},{3,2},{4,5},{5,4},{6,7},{7,6},{8,9},{9,8},{10,11... | collective-permute-start | bytes 3145736 | tf_op jit(solution)/shard_map/ppermute | solution.py:377
  33.7 2.7 %collective-permute-start = (f32[8,128]{1,0:T(8,128)S(1)}, f32[8,128]{1,0:T(8,128)S(1)}, u32[]{:S(2)}, u32[]{:S(2)}) collective-permute-start(f32[8,128]{1,0:T(8,128)S(1)} %get-tuple-element.16), channel_id=1, source_target_pairs={{0,1},{1,0},{2,3},{3,2},{4,5},{5,4},{6,7},{7,6},{8,9},{9,8},{10,11... | collective-permute-start | bytes 12296 | tf_op jit(solution)/shard_map/ppermute | solution.py:377
  37.5 15.3 %collective-permute-start.2 = (bf16[2064,128]{1,0:T(8,128)(2,1)S(1)}, bf16[2064,128]{1,0:T(8,128)(2,1)S(1)}, u32[]{:S(2)}, u32[]{:S(2)}) collective-permute-start(bf16[2064,128]{1,0:T(8,128)(2,1)S(1)} %get-tuple-element.19), channel_id=1, source_target_pairs={{0,96},{96,0},{32,64},{64,32},{1,97},{97,1},{33,65},{65,33},{2,98}... | collective-permute-start | bytes 1585160 | tf_op jit(solution)/shard_map/ppermute | solution.py:381
  53.0 5.0 %collective-permute-start.4 = (bf16[2064,128]{1,0:T(8,128)(2,1)S(1)}, bf16[2064,128]{1,0:T(8,128)(2,1)S(1)}, u32[]{:S(2)}, u32[]{:S(2)}) collective-permute-start(bf16[2064,128]{1,0:T(8,128)(2,1)S(1)} %add_convert_fusion.half_ref), channel_id=1, source_target_pairs={{0,1},{1,0},{2,3},{3,2},{4,5},{5,4},{6,7},{7,6},{8,9},{9,8},{10,11... | collective-permute-start | bytes 1585160 | tf_op jit(solution)/shard_map/ppermute | solution.py:377
  53.1 4.9 %collective-permute-start.3 = (f32[8,128]{1,0:T(8,128)S(1)}, f32[8,128]{1,0:T(8,128)S(1)}, u32[]{:S(2)}, u32[]{:S(2)}) collective-permute-start(f32[8,128]{1,0:T(8,128)S(1)} %reduce_sum.18), channel_id=1, source_target_pairs={{0,96},{96,0},{32,64},{64,32},{1,97},{97,1},{33,65},{65,33},{2,98}... | collective-permute-start | bytes 12296 | tf_op jit(solution)/shard_map/ppermute | solution.py:381

commit v8 on v5

--- a/solution.py
+++ b/solution.py
@@ -321,12 +321,16 @@
         for at in columns:
             yield at, mxu(field(), gram[:, at], ((1,), (0,)))
 
-    vector = jnp.full((1, width), 1.0 / width**0.5, jnp.float32)
-    for _ in range(power_steps):
-        image = mxu(as_three(vector), gram[...], ((1,), (0,)))
-        image = jnp.sum(image, axis=0, keepdims=True)
-        radius = jnp.sqrt(jnp.sum(image * image, axis=1, keepdims=True) + 1e-06)
-        vector = image / radius
+    def image_of(vector):
+        return jnp.sum(mxu(as_three(vector), gram[...], ((1,), (0,))), axis=0, keepdims=True)
+
+    def size_of(image):
+        return jnp.sqrt(jnp.sum(image * image, axis=1, keepdims=True) + 1e-06)
+
+    image = image_of(jnp.full((1, width), 1.0 / width**0.5, jnp.float32))
+    for _ in range(1, power_steps):
+        image = image_of(image) * (1.0 / size_of(image))
+    radius = size_of(image)
     total = jnp.sum(sum_ref[0:1, :], axis=1, keepdims=True) + jnp.sum(
         jnp.sum(far_sum_ref[...].astype(jnp.float32)[0:3, :], axis=0, keepdims=True),
         axis=1,
@@ -337,11 +341,10 @@
     strides = [1.0 / center]
     momenta = []
     for sweep in range(1, ITERS):
-        if sweep == 1:
-            momenta.append(0.5 * (radius * strides[-1]) ** 2)
-        else:
-            momenta.append((0.5 * radius * strides[-1]) ** 2)
-        strides.append(1.0 / (center - momenta[-1] / strides[-1]))
+        ratio = radius * strides[-1]
+        factor = 0.5 if sweep == 1 else 0.25
+        momenta.append(factor * ratio * ratio)
+        strides.append(1.0 / (center - factor * radius * ratio))
     keep = [1.0 + m - s * damping for m, s in zip(momenta, strides)]
     weights = (
         strides[1] - strides[3] * momenta[1],

time: 78.6 us -> 78.3 us (level)
  no operation moved by 1% of the time
where the time goes in v8:
time: 78.3 us; the launch traced here: 78.1 us
  blocking collectives  43.6 us (56%)
  Pallas kernels  15.6 us (20%)
  waiting for transfers between devices  14.4 us (18%)
  starting transfers between devices  3.49 us (4%)
  other arithmetic  0.84 us (1%)
    all_to_all x1, blocking collectives, shards(): arrived = lax.all_to_all(by_block, OWNERS, 0, 0, tiled=True)  28.2 us
    all_to_all x1, blocking collectives, shards(): lax.all_to_all(term.reshape(blocks, examples, -1), OWNERS, 0, 0, tiled=True)  15.4 us
    ppermute x2, waiting for transfers between devices, to_other_owner(): lax.ppermute(value, ('side', 'pair'), [(0, 3), (3, 0), (1, 2), (2, 1)])  11.3 us
    pallas_call x1, Pallas kernels, features_of(): pl.pallas_call(feature_kernel, grid=(steps,), in_specs=[pl.BlockSpec(memo...  8.04 us
    pallas_call x1, Pallas kernels, block_scores(): pl.pallas_call(functools.partial(solve_kernel, coords), in_specs=[smem] +...  5.16 us
    ppermute x2, starting transfers between devices, to_other_owner(): lax.ppermute(value, ('side', 'pair'), [(0, 3), (3, 0), (1, 2), (2, 1)])  3.32 us
    ppermute x3, waiting for transfers between devices, shifted(): lax.ppermute(value, axis, [(i, (i + shift) % size) for i in range(size)])  3.18 us
  transfers between devices with their start and end apart: 5, of which 4 were waited for; matrix products, arithmetic and copies ran while one was open for 0% of the time, Pallas kernels for 2%

profile of v8, /device:TPU:0, one launch (start us, length us, event | category | flops | bytes accessed | tf_op | source)
XLA Modules:
  0.0 78.1 jit_solution(11714404162636017946)
XLA Ops:
  0.0 8.0 %features.1 = bf16[32,16,1152]{2,1,0:T(8,128)(2,1)S(1)} custom-call(s32[1]{0:T(128)} %bitcast.1.side_ref, bf16[1024,3072]{1,0:T(8,128)(2,1)} %act_ref.1, bf16[1024,3072]{1,0:T(8,128)(2,1)} %grad_ref.1, bf16[3072,128]{1,0:T(8,128)(2,1)} %pa_ref.1, bf16[3072,256]{1,0:T(8,128)(2,1)} %po_ref.1), custom_call_target="tpu_custom_call" | custom-call | tf_op jit(solution)/shard_map/features/pallas_call | solution.py:90
  8.1 28.2 %all_to_all.10 = bf16[32,16,1152]{2,1,0:T(8,128)(2,1)S(1)} all-to-all(bf16[32,16,1152]{2,1,0:T(8,128)(2,1)S(1)} %features.1), channel_id=1, replica_groups=mesh['side'=2,'pair'=2,'blk_0'=4,'blk_1'=4,'core'=2] {'pair','blk_0','bl..., dimensions={0} | all-to-all | bytes 2359296 | tf_op jit(solution)/shard_map/all_to_all | solution.py:423
  36.3 0.0 collective-permute-start
  36.3 0.6 own_gram.1.acc_ref
  36.9 2.3 %collective-permute-done.other_ref = bf16[512,1152]{1,0:T(8,128)(2,1)S(1)} collective-permute-done((bf16[512,1152]{1,0:T(8,128)(2,1)S(1)}, bf16[512,1152]{1,0:T(8,128)(2,1)S(1)}, u32[]{:S(2)}, u32[]{:S(2)}) %collective-permute-start) | collective-permute-done | bytes 1179680 | tf_op jit(solution)/shard_map/ppermute | solution.py:410
  39.1 0.6 gram_parts.1
  39.7 2.0 %collective-permute-start.1 = (bf16[1040,128]{1,0:T(8,128)(2,1)S(1)}, bf16[1040,128]{1,0:T(8,128)(2,1)S(1)}, u32[]{:S(2)}, u32[]{:S(2)}) collective-permute-start(bf16[1040,128]{1,0:T(8,128)(2,1)S(1)} %get-tuple-element.16), channel_id=1, source_target_pairs={{0,96},{96,0},{32,64},{64,32},{1,97},{97,1},{33,65},{65,33},{2,98}... | collective-permute-start | bytes 798728 | tf_op jit(solution)/shard_map/ppermute | solution.py:414
  41.7 1.3 %collective-permute-start.2 = (bf16[1040,128]{1,0:T(8,128)(2,1)S(1)}, bf16[1040,128]{1,0:T(8,128)(2,1)S(1)}, u32[]{:S(2)}, u32[]{:S(2)}) collective-permute-start(bf16[1040,128]{1,0:T(8,128)(2,1)S(1)} %get-tuple-element.18), channel_id=1, source_target_pairs={{0,96},{96,0},{32,64},{64,32},{1,97},{97,1},{33,65},{65,33},{2,98}... | collective-permute-start | bytes 798728 | tf_op jit(solution)/shard_map/ppermute | solution.py:414
  43.0 7.2 %collective-permute-done.1 = bf16[1040,128]{1,0:T(8,128)(2,1)S(1)} collective-permute-done((bf16[1040,128]{1,0:T(8,128)(2,1)S(1)}, bf16[1040,128]{1,0:T(8,128)(2,1)S(1)}, u32[]{:S(2)}, u32[]{:S(2)}) %collective-permute-start.1) | collective-permute-done | bytes 266272 | tf_op jit(solution)/shard_map/ppermute | solution.py:414
  50.2 0.1 add_convert_fusion.half_ref
  50.3 0.1 collective-permute-start.4
  50.4 0.7 in_order.1.group_ref
  51.1 4.0 %collective-permute-done.2 = bf16[1040,128]{1,0:T(8,128)(2,1)S(1)} collective-permute-done((bf16[1040,128]{1,0:T(8,128)(2,1)S(1)}, bf16[1040,128]{1,0:T(8,128)(2,1)S(1)}, u32[]{:S(2)}, u32[]{:S(2)}) %collective-permute-start.2) | collective-permute-done | bytes 266272 | tf_op jit(solution)/shard_map/ppermute | solution.py:414
  55.1 0.1 add_convert_fusion.1.half_ref
  55.2 0.1 collective-permute-start.3
  55.3 0.0 collective-permute-done.4.rest_ref
  55.3 0.4 spread.1.started_ref
  55.7 0.2 spread_on.1.started_ref
  55.9 0.9 %collective-permute-done.3.rest_ref = bf16[1040,128]{1,0:T(8,128)(2,1)S(1)} collective-permute-done((bf16[1040,128]{1,0:T(8,128)(2,1)S(1)}, bf16[1040,128]{1,0:T(8,128)(2,1)S(1)}, u32[]{:S(2)}, u32[]{:S(2)}) %collective-permute-start.3) | collective-permute-done | bytes 266272 | tf_op jit(solution)/shard_map/ppermute | solution.py:410
  56.8 5.2 %solve.1 = (bf16[512,512]{1,0:T(8,128)(2,1)S(1)}, bf16[1024,1024]{1,0:T(8,128)(2,1)S(1)}) custom-call(s32[1]{0:T(128)} %bitcast.core_ref, f32[8,128]{1,0:T(8,128)S(1)} %get-tuple-element.15.sum_ref, bf16[16,128]{1,0:T(8,128)(2,1)S(1)} %slice.9.far_sum_ref, bf16[1040,128]{1,0:T(8,128)(2,1)S(1)} %collective-permute-done.3.rest_ref, ...), custom_call_target="tpu_custom_call", output_to_operand_aliasing={{1}: (4, {})} | custom-call | tf_op jit(solution)/shard_map/solve/pallas_call | solution.py:389
  62.0 15.4 %all_to_all.11 = bf16[32,16,512]{2,1,0:T(8,128)(2,1)S(1)} all-to-all(bf16[32,16,512]{2,1,0:T(8,128)(2,1)S(1)} %bitcast.9), channel_id=1, replica_groups=mesh['side'=2,'pair'=2,'blk_0'=4,'blk_1'=4,'core'=2] {'pair','blk_0','bl..., dimensions={0} | all-to-all | bytes 1048576 | tf_op jit(solution)/shard_map/all_to_all | solution.py:443
  77.4 0.1 convert_reduce_fusion
  77.5 0.6 broadcast_multiply_fusion
  (2 shorter events, 0.0 us)
Async XLA Ops:
  36.3 2.8 %collective-permute-start = (bf16[512,1152]{1,0:T(8,128)(2,1)S(1)}, bf16[512,1152]{1,0:T(8,128)(2,1)S(1)}, u32[]{:S(2)}, u32[]{:S(2)}) collective-permute-start(bf16[512,1152]{1,0:T(8,128)(2,1)S(1)} %bitcast.4), channel_id=1, source_target_pairs={{0,1},{1,0},{2,3},{3,2},{4,5},{5,4},{6,7},{7,6},{8,9},{9,8},{10,11... | collective-permute-start | bytes 3538952 | tf_op jit(solution)/shard_map/ppermute | solution.py:410
  39.7 10.5 %collective-permute-start.1 = (bf16[1040,128]{1,0:T(8,128)(2,1)S(1)}, bf16[1040,128]{1,0:T(8,128)(2,1)S(1)}, u32[]{:S(2)}, u32[]{:S(2)}) collective-permute-start(bf16[1040,128]{1,0:T(8,128)(2,1)S(1)} %get-tuple-element.16), channel_id=1, source_target_pairs={{0,96},{96,0},{32,64},{64,32},{1,97},{97,1},{33,65},{65,33},{2,98}... | collective-permute-start | bytes 798728 | tf_op jit(solution)/shard_map/ppermute | solution.py:414
  41.7 13.4 %collective-permute-start.2 = (bf16[1040,128]{1,0:T(8,128)(2,1)S(1)}, bf16[1040,128]{1,0:T(8,128)(2,1)S(1)}, u32[]{:S(2)}, u32[]{:S(2)}) collective-permute-start(bf16[1040,128]{1,0:T(8,128)(2,1)S(1)} %get-tuple-element.18), channel_id=1, source_target_pairs={{0,96},{96,0},{32,64},{64,32},{1,97},{97,1},{33,65},{65,33},{2,98}... | collective-permute-start | bytes 798728 | tf_op jit(solution)/shard_map/ppermute | solution.py:414
  50.3 5.0 %collective-permute-start.4 = (bf16[1040,128]{1,0:T(8,128)(2,1)S(1)}, bf16[1040,128]{1,0:T(8,128)(2,1)S(1)}, u32[]{:S(2)}, u32[]{:S(2)}) collective-permute-start(bf16[1040,128]{1,0:T(8,128)(2,1)S(1)} %add_convert_fusion.half_ref), channel_id=1, source_target_pairs={{0,1},{1,0},{2,3},{3,2},{4,5},{5,4},{6,7},{7,6},{8,9},{9,8},{10,11... | collective-permute-start | bytes 798728 | tf_op jit(solution)/shard_map/ppermute | solution.py:410
  55.2 1.6 %collective-permute-start.3 = (bf16[1040,128]{1,0:T(8,128)(2,1)S(1)}, bf16[1040,128]{1,0:T(8,128)(2,1)S(1)}, u32[]{:S(2)}, u32[]{:S(2)}) collective-permute-start(bf16[1040,128]{1,0:T(8,128)(2,1)S(1)} %add_convert_fusion.1.half_ref), channel_id=1, source_target_pairs={{0,1},{1,0},{2,3},{3,2},{4,5},{5,4},{6,7},{7,6},{8,9},{9,8},{10,11... | collective-permute-start | bytes 798728 | tf_op jit(solution)/shard_map/ppermute | solution.py:410

commit v9 on v8

--- a/solution.py
+++ b/solution.py
@@ -299,6 +299,7 @@
 
 def solve_kernel(
     coords,
+    scale,
     core_ref,
     sum_ref,
     far_sum_ref,
@@ -347,10 +348,11 @@
         strides.append(1.0 / (center - factor * radius * ratio))
     keep = [1.0 + m - s * damping for m, s in zip(momenta, strides)]
     weights = (
-        strides[1] - strides[3] * momenta[1],
-        strides[2] + strides[3] * keep[2],
-        strides[3] * strides[2],
+        scale * (strides[1] - strides[3] * momenta[1]),
+        scale * (strides[2] + strides[3] * keep[2]),
+        scale * (strides[3] * strides[2]),
     )
+    start = scale * strides[0]
 
     def right_side(at):
         return mine_ref[:, at].astype(jnp.float32)
@@ -365,7 +367,7 @@
         low[1, :, at] = value.astype(jnp.bfloat16)
     for at, value in operate(lambda: low[1]):
         value = (
-            strides[0] * right_side(at)
+            start * right_side(at)
             + weights[0] * first[:, at]
             + weights[1] * second[:, at]
             - weights[2] * value
@@ -380,14 +382,14 @@
         ).astype(out_ref.dtype)
 
 
-def block_scores(coords, core, squares, far_squares, rest, started, mine, rows):
+def block_scores(coords, scale, core, squares, far_squares, rest, started, mine, rows):
     vmem = pl.BlockSpec(memory_space=pltpu.VMEM)
     smem = pl.BlockSpec(memory_space=pltpu.SMEM)
     examples = mine.shape[0]
     width = started.shape[0]
     field = (examples, width)
     return pl.pallas_call(
-        functools.partial(solve_kernel, coords),
+        functools.partial(solve_kernel, coords, scale),
         in_specs=[smem] + [vmem] * 6,
         out_specs=[vmem, vmem],
         out_shape=[
@@ -439,10 +441,10 @@
     rest_b = shifted(half_b, "core", 1)
     started = spread_on(core, half_b, started)
     far_squares = across_a[across_a.shape[0] - 16 :]
-    term = block_scores(coords, core, squares, far_squares, rest_b, started, mine, rows)
+    scale = float(examples * lax.axis_size(("side", "pair")))
+    term = block_scores(coords, scale, core, squares, far_squares, rest_b, started, mine, rows)
     terms = lax.all_to_all(term.reshape(blocks, examples, -1), OWNERS, 0, 0, tiled=True)
-    scores = jnp.sum(terms.astype(jnp.float32), axis=0)
-    return scores * float(examples * lax.axis_size(("side", "pair")))
+    return jnp.sum(terms.astype(jnp.float32), axis=0)
 
 
 def solution(mesh):

time: 78.3 us -> 78.3 us (level)
  no operation moved by 1% of the time
where the time goes in v9:
time: 78.3 us; the launch traced here: 78.1 us
  blocking collectives  43.6 us (56%)
  Pallas kernels  15.6 us (20%)
  waiting for transfers between devices  14.4 us (18%)
  starting transfers between devices  3.49 us (4%)
  other arithmetic  0.83 us (1%)
    all_to_all x1, blocking collectives, shards(): arrived = lax.all_to_all(by_block, OWNERS, 0, 0, tiled=True)  28.2 us
    all_to_all x1, blocking collectives, shards(): lax.all_to_all(term.reshape(blocks, examples, -1), OWNERS, 0, 0, tiled=True)  15.4 us
    ppermute x2, waiting for transfers between devices, to_other_owner(): lax.ppermute(value, ('side', 'pair'), [(0, 3), (3, 0), (1, 2), (2, 1)])  11.3 us
    pallas_call x1, Pallas kernels, features_of(): pl.pallas_call(feature_kernel, grid=(steps,), in_specs=[pl.BlockSpec(memo...  8.04 us
    pallas_call x1, Pallas kernels, block_scores(): pl.pallas_call(functools.partial(solve_kernel, coords, scale), in_specs=[...  5.16 us
    ppermute x2, starting transfers between devices, to_other_owner(): lax.ppermute(value, ('side', 'pair'), [(0, 3), (3, 0), (1, 2), (2, 1)])  3.32 us
    ppermute x3, waiting for transfers between devices, shifted(): lax.ppermute(value, axis, [(i, (i + shift) % size) for i in range(size)])  3.18 us
  transfers between devices with their start and end apart: 5, of which 4 were waited for; matrix products, arithmetic and copies ran while one was open for 0% of the time, Pallas kernels for 2%

profile of v9, /device:TPU:0, one launch (start us, length us, event | category | flops | bytes accessed | tf_op | source)
XLA Modules:
  0.0 78.1 jit_solution(229714621777096369)
XLA Ops:
  0.0 8.0 %features.1 = bf16[32,16,1152]{2,1,0:T(8,128)(2,1)S(1)} custom-call(s32[1]{0:T(128)} %bitcast.1.side_ref, bf16[1024,3072]{1,0:T(8,128)(2,1)} %act_ref.1, bf16[1024,3072]{1,0:T(8,128)(2,1)} %grad_ref.1, bf16[3072,128]{1,0:T(8,128)(2,1)} %pa_ref.1, bf16[3072,256]{1,0:T(8,128)(2,1)} %po_ref.1), custom_call_target="tpu_custom_call" | custom-call | tf_op jit(solution)/shard_map/features/pallas_call | solution.py:90
  8.1 28.2 %all_to_all.10 = bf16[32,16,1152]{2,1,0:T(8,128)(2,1)S(1)} all-to-all(bf16[32,16,1152]{2,1,0:T(8,128)(2,1)S(1)} %features.1), channel_id=1, replica_groups=mesh['side'=2,'pair'=2,'blk_0'=4,'blk_1'=4,'core'=2] {'pair','blk_0','bl..., dimensions={0} | all-to-all | bytes 2359296 | tf_op jit(solution)/shard_map/all_to_all | solution.py:425
  36.3 0.0 collective-permute-start
  36.3 0.6 own_gram.1.acc_ref
  36.9 2.3 %collective-permute-done.other_ref = bf16[512,1152]{1,0:T(8,128)(2,1)S(1)} collective-permute-done((bf16[512,1152]{1,0:T(8,128)(2,1)S(1)}, bf16[512,1152]{1,0:T(8,128)(2,1)S(1)}, u32[]{:S(2)}, u32[]{:S(2)}) %collective-permute-start) | collective-permute-done | bytes 1179680 | tf_op jit(solution)/shard_map/ppermute | solution.py:412
  39.1 0.6 gram_parts.1
  39.7 2.0 %collective-permute-start.1 = (bf16[1040,128]{1,0:T(8,128)(2,1)S(1)}, bf16[1040,128]{1,0:T(8,128)(2,1)S(1)}, u32[]{:S(2)}, u32[]{:S(2)}) collective-permute-start(bf16[1040,128]{1,0:T(8,128)(2,1)S(1)} %get-tuple-element.16), channel_id=1, source_target_pairs={{0,96},{96,0},{32,64},{64,32},{1,97},{97,1},{33,65},{65,33},{2,98}... | collective-permute-start | bytes 798728 | tf_op jit(solution)/shard_map/ppermute | solution.py:416
  41.7 1.3 %collective-permute-start.2 = (bf16[1040,128]{1,0:T(8,128)(2,1)S(1)}, bf16[1040,128]{1,0:T(8,128)(2,1)S(1)}, u32[]{:S(2)}, u32[]{:S(2)}) collective-permute-start(bf16[1040,128]{1,0:T(8,128)(2,1)S(1)} %get-tuple-element.18), channel_id=1, source_target_pairs={{0,96},{96,0},{32,64},{64,32},{1,97},{97,1},{33,65},{65,33},{2,98}... | collective-permute-start | bytes 798728 | tf_op jit(solution)/shard_map/ppermute | solution.py:416
  43.0 7.2 %collective-permute-done.1 = bf16[1040,128]{1,0:T(8,128)(2,1)S(1)} collective-permute-done((bf16[1040,128]{1,0:T(8,128)(2,1)S(1)}, bf16[1040,128]{1,0:T(8,128)(2,1)S(1)}, u32[]{:S(2)}, u32[]{:S(2)}) %collective-permute-start.1) | collective-permute-done | bytes 266272 | tf_op jit(solution)/shard_map/ppermute | solution.py:416
  50.2 0.1 add_convert_fusion.half_ref
  50.3 0.1 collective-permute-start.4
  50.4 0.7 in_order.1.group_ref
  51.1 4.0 %collective-permute-done.2 = bf16[1040,128]{1,0:T(8,128)(2,1)S(1)} collective-permute-done((bf16[1040,128]{1,0:T(8,128)(2,1)S(1)}, bf16[1040,128]{1,0:T(8,128)(2,1)S(1)}, u32[]{:S(2)}, u32[]{:S(2)}) %collective-permute-start.2) | collective-permute-done | bytes 266272 | tf_op jit(solution)/shard_map/ppermute | solution.py:416
  55.1 0.1 add_convert_fusion.1.half_ref
  55.2 0.1 collective-permute-start.3
  55.3 0.0 collective-permute-done.4.rest_ref
  55.3 0.4 spread.1.started_ref
  55.7 0.2 spread_on.1.started_ref
  55.9 0.9 %collective-permute-done.3.rest_ref = bf16[1040,128]{1,0:T(8,128)(2,1)S(1)} collective-permute-done((bf16[1040,128]{1,0:T(8,128)(2,1)S(1)}, bf16[1040,128]{1,0:T(8,128)(2,1)S(1)}, u32[]{:S(2)}, u32[]{:S(2)}) %collective-permute-start.3) | collective-permute-done | bytes 266272 | tf_op jit(solution)/shard_map/ppermute | solution.py:412
  56.8 5.2 %solve.1 = (bf16[512,512]{1,0:T(8,128)(2,1)S(1)}, bf16[1024,1024]{1,0:T(8,128)(2,1)S(1)}) custom-call(s32[1]{0:T(128)} %bitcast.core_ref, f32[8,128]{1,0:T(8,128)S(1)} %get-tuple-element.15.sum_ref, bf16[16,128]{1,0:T(8,128)(2,1)S(1)} %slice.9.far_sum_ref, bf16[1040,128]{1,0:T(8,128)(2,1)S(1)} %collective-permute-done.3.rest_ref, ...), custom_call_target="tpu_custom_call", output_to_operand_aliasing={{1}: (4, {})} | custom-call | tf_op jit(solution)/shard_map/solve/pallas_call | solution.py:391
  62.0 15.4 %all_to_all.11 = bf16[32,16,512]{2,1,0:T(8,128)(2,1)S(1)} all-to-all(bf16[32,16,512]{2,1,0:T(8,128)(2,1)S(1)} %bitcast.9), channel_id=1, replica_groups=mesh['side'=2,'pair'=2,'blk_0'=4,'blk_1'=4,'core'=2] {'pair','blk_0','bl..., dimensions={0} | all-to-all | bytes 1048576 | tf_op jit(solution)/shard_map/all_to_all | solution.py:446
  77.4 0.7 convert_reduce_fusion
  (2 shorter events, 0.0 us)
Async XLA Ops:
  36.3 2.8 %collective-permute-start = (bf16[512,1152]{1,0:T(8,128)(2,1)S(1)}, bf16[512,1152]{1,0:T(8,128)(2,1)S(1)}, u32[]{:S(2)}, u32[]{:S(2)}) collective-permute-start(bf16[512,1152]{1,0:T(8,128)(2,1)S(1)} %bitcast.4), channel_id=1, source_target_pairs={{0,1},{1,0},{2,3},{3,2},{4,5},{5,4},{6,7},{7,6},{8,9},{9,8},{10,11... | collective-permute-start | bytes 3538952 | tf_op jit(solution)/shard_map/ppermute | solution.py:412
  39.7 10.5 %collective-permute-start.1 = (bf16[1040,128]{1,0:T(8,128)(2,1)S(1)}, bf16[1040,128]{1,0:T(8,128)(2,1)S(1)}, u32[]{:S(2)}, u32[]{:S(2)}) collective-permute-start(bf16[1040,128]{1,0:T(8,128)(2,1)S(1)} %get-tuple-element.16), channel_id=1, source_target_pairs={{0,96},{96,0},{32,64},{64,32},{1,97},{97,1},{33,65},{65,33},{2,98}... | collective-permute-start | bytes 798728 | tf_op jit(solution)/shard_map/ppermute | solution.py:416
  41.7 13.4 %collective-permute-start.2 = (bf16[1040,128]{1,0:T(8,128)(2,1)S(1)}, bf16[1040,128]{1,0:T(8,128)(2,1)S(1)}, u32[]{:S(2)}, u32[]{:S(2)}) collective-permute-start(bf16[1040,128]{1,0:T(8,128)(2,1)S(1)} %get-tuple-element.18), channel_id=1, source_target_pairs={{0,96},{96,0},{32,64},{64,32},{1,97},{97,1},{33,65},{65,33},{2,98}... | collective-permute-start | bytes 798728 | tf_op jit(solution)/shard_map/ppermute | solution.py:416
  50.3 5.0 %collective-permute-start.4 = (bf16[1040,128]{1,0:T(8,128)(2,1)S(1)}, bf16[1040,128]{1,0:T(8,128)(2,1)S(1)}, u32[]{:S(2)}, u32[]{:S(2)}) collective-permute-start(bf16[1040,128]{1,0:T(8,128)(2,1)S(1)} %add_convert_fusion.half_ref), channel_id=1, source_target_pairs={{0,1},{1,0},{2,3},{3,2},{4,5},{5,4},{6,7},{7,6},{8,9},{9,8},{10,11... | collective-permute-start | bytes 798728 | tf_op jit(solution)/shard_map/ppermute | solution.py:412
  55.2 1.6 %collective-permute-start.3 = (bf16[1040,128]{1,0:T(8,128)(2,1)S(1)}, bf16[1040,128]{1,0:T(8,128)(2,1)S(1)}, u32[]{:S(2)}, u32[]{:S(2)}) collective-permute-start(bf16[1040,128]{1,0:T(8,128)(2,1)S(1)} %add_convert_fusion.1.half_ref), channel_id=1, source_target_pairs={{0,1},{1,0},{2,3},{3,2},{4,5},{5,4},{6,7},{7,6},{8,9},{9,8},{10,11... | collective-permute-start | bytes 798728 | tf_op jit(solution)/shard_map/ppermute | solution.py:412
